TPU v7x, 128 devices: a whole 4x4x4 slice. The times are simulated.
128 devices in a mesh: pool: 8 (over x, y_lo), expert: 16 (over y_hi, z, core).
Axes of the slice: x: 4, y: 4 (y_hi: 2, y_lo: 2; y = y_hi * 2 + y_lo), z: 4, core: 2. Of those that a mesh axis runs over, the one named last changes fastest.
Arguments:
- queries: bfloat16 [4096, 4096], P(('pool', 'expert')), may hold values from -6 to 6
- kv_cache: bfloat16 [4096, 64, 1024], P(('pool', 'expert')), may hold values from -6 to 6
- block_index: int32 [4096, 8], P(('pool', 'expert')), may hold values from 0 to 31, as said below
- lengths: int32 [4096], P(('pool', 'expert')), may hold values from 2 to 512, as said below
- residual: bfloat16 [4096, 2048], P('pool', 'expert'), may hold values from -21 to 21
- out_weight: bfloat16 [4096, 2048], P(None, 'expert'), may hold values from -0.09375 to 0.09375
- norm_gain: float32 [2048], P('expert'), may hold values from 0.25 to 1.75
- expert_ids: int32 [4096, 8], P('pool'), may hold values from 0 to 127, all different within a row; in each aligned block of 512 rows (0 to 511, 512 to 1023, ...) at most 64 rows name the same one
- route_weights: float32 [4096, 8], P('pool'), may hold values from 0.02 to 0.25
- gate_weight: bfloat16 [128, 2048, 768], P(('pool', 'expert')), may hold values from -0.125 to 0.125
- up_weight: bfloat16 [128, 2048, 768], P(('pool', 'expert')), may hold values from -0.125 to 0.125
- down_weight: bfloat16 [128, 768, 2048], P(('pool', 'expert')), may hold values from -0.21875 to 0.21875
Outputs:
- attended: bfloat16 [4096, 2048], P('pool', 'expert')
- expert_mix: bfloat16 [4096, 2048], P('pool', 'expert')
Inputs may be any that keep to these rules, and one draw needn't show every extreme that they name: Sequence t reads blocks of the pool of 32 blocks held with it: block (t // 32) * 32 + block_index[t, j] of kv_cache. The first lengths[t] of the sequence's 8 * 64 positions are live. `expert_ids`: each row names 8 different experts; within the 512 rows of one index of pool no expert is named by more than 64 rows.
All inputs are finite; a program needn't handle non-finite values.
Results may differ from a plain program's by a relative error of at most 0.01.
Values may be sent and summed in bfloat16 or wider, within the bound.
A program may use at most 128 MiB of HBM per device.

v0:
```python
import jax
import jax.numpy as jnp
from jax import lax
from jax.sharding import PartitionSpec as P

HEAD_DIM = 128


epsilon = 1e-06


def sent_to_all(value, axis):
    size = lax.axis_size(axis)
    return lax.all_to_all(
        jnp.broadcast_to(value[None], (size, *value.shape)), axis, 0, 0, tiled=True
    )


def taken_together(value, axis):
    everything = sent_to_all(value, axis)
    return jnp.sum(everything, axis=0)


def shards(
    queries,
    kv_cache,
    block_index,
    lengths,
    residual,
    out_weight,
    norm_gain,
    expert_ids,
    route_weights,
    gate_weight,
    up_weight,
    down_weight,
):
    rows_dev = queries.shape[0]
    pool_blocks, block_len, kv_width = kv_cache.shape
    blocks_row = block_index.shape[1]
    context = blocks_row * block_len
    kv_half = kv_width // 2
    kv_heads = kv_half // HEAD_DIM
    head_count = queries.shape[1] // HEAD_DIM
    group_size = head_count // kv_heads
    step_rows = 4
    kv_flat = kv_cache.reshape(pool_blocks, block_len * kv_width)
    positions = jnp.arange(context, dtype=jnp.int32)
    block_ids = jnp.arange(pool_blocks, dtype=jnp.int32)

    def attend(inputs):
        query_rows, index_rows, length_rows = inputs
        selector = (index_rows.reshape(-1)[:, None] == block_ids[None, :]).astype(jnp.bfloat16)
        gathered = jnp.dot(selector, kv_flat, preferred_element_type=jnp.bfloat16)
        gathered = gathered.reshape(step_rows, context, kv_width)
        key_part = gathered[:, :, :kv_half].reshape(step_rows, context, kv_heads, HEAD_DIM)
        value_part = gathered[:, :, kv_half:].reshape(step_rows, context, kv_heads, HEAD_DIM)
        query_split = query_rows.reshape(step_rows, kv_heads, group_size, HEAD_DIM)
        scores = jnp.einsum(
            "rgqd,rpgd->rgqp", query_split, key_part, preferred_element_type=jnp.float32
        ) * HEAD_DIM ** (-0.5)
        live_mask = positions[None, :] < length_rows[:, None]
        scores = jnp.where(live_mask[:, None, None, :], scores, -1e30)
        maximum = jnp.max(scores, axis=-1, keepdims=True)
        exponent = jnp.exp(scores - maximum)
        softmax_w = (exponent / jnp.sum(exponent, axis=-1, keepdims=True)).astype(jnp.bfloat16)
        attended_part = jnp.einsum(
            "rgqp,rpgd->rgqd", softmax_w, value_part, preferred_element_type=jnp.float32
        )
        return attended_part.astype(jnp.bfloat16).reshape(step_rows, head_count * HEAD_DIM)

    attention = lax.map(
        attend,
        (
            queries.reshape(rows_dev // step_rows, step_rows, -1),
            block_index.reshape(rows_dev // step_rows, step_rows, blocks_row),
            lengths.reshape(rows_dev // step_rows, step_rows),
        ),
    )
    attention = attention.reshape(rows_dev, head_count * HEAD_DIM)
    expert_size = lax.axis_size("expert")
    col_width = out_weight.shape[1]
    full_width = col_width * expert_size
    proj_rows = jnp.dot(
        attention,
        lax.all_gather(out_weight, "expert", axis=1, tiled=True),
        preferred_element_type=jnp.float32,
    )
    projected = lax.all_to_all(proj_rows, "expert", split_axis=1, concat_axis=0, tiled=True)
    attended = (residual.astype(jnp.float32) + projected).astype(jnp.bfloat16)
    attended_f = attended.astype(jnp.float32)
    part_sq = jnp.sum(attended_f * attended_f, axis=1)
    square_sum = taken_together(part_sq, "expert")
    inverse_rms = lax.rsqrt(square_sum / full_width + epsilon)
    normed = (attended_f * inverse_rms[:, None] * norm_gain[None, :]).astype(jnp.bfloat16)
    group_rows, top_count = expert_ids.shape
    pool_size = lax.axis_size("pool")
    device_count = pool_size * expert_size
    local_count = gate_weight.shape[0]
    hidden_width = gate_weight.shape[2]
    experts = device_count * local_count
    capacity = 2 * group_rows * top_count // experts
    flat_ids = expert_ids.reshape(-1)
    onehot = (flat_ids[:, None] == jnp.arange(experts, dtype=jnp.int32)[None, :]).astype(jnp.int32)
    before = jnp.cumsum(onehot, axis=0) - onehot
    slot_ids = jnp.sum(before * onehot, axis=1)
    owner_dev = flat_ids // local_count
    within = flat_ids % local_count
    destination = ((owner_dev * capacity + slot_ids) * local_count + within).reshape(
        group_rows, top_count
    )
    slot_span = experts * capacity
    slots_all = jnp.arange(slot_span, dtype=jnp.int32)
    chosen = jnp.zeros((group_rows, slot_span), jnp.bfloat16)
    for position in range(top_count):
        chosen = chosen + (destination[:, position : position + 1] == slots_all[None, :]).astype(
            jnp.bfloat16
        )
    outgoing = lax.dot_general(
        chosen, normed, (((0,), (0,)), ((), ())), preferred_element_type=jnp.bfloat16
    )
    gate_split = gate_weight.reshape(local_count, expert_size, col_width, hidden_width)
    up_split = up_weight.reshape(local_count, expert_size, col_width, hidden_width)
    down_split = down_weight.reshape(local_count, hidden_width, expert_size, col_width)
    received = lax.all_to_all(
        outgoing.reshape(device_count, capacity, local_count, col_width),
        ("pool", "expert"),
        split_axis=0,
        concat_axis=0,
        tiled=True,
    )
    item_count = received.shape[1]
    shaped = received.reshape(pool_size, expert_size, item_count, local_count, col_width)
    gate_act = jnp.einsum(
        "peixc,xecf->xpif", shaped, gate_split, preferred_element_type=jnp.float32
    )
    upper = jnp.einsum("peixc,xecf->xpif", shaped, up_split, preferred_element_type=jnp.float32)
    hidden = (jax.nn.silu(gate_act) * upper).astype(jnp.bfloat16)
    result = (
        jnp.einsum("xpif,xfec->peixc", hidden, down_split, preferred_element_type=jnp.float32)
        .astype(jnp.bfloat16)
        .reshape(device_count, item_count, local_count, col_width)
    )
    returned = lax.all_to_all(result, ("pool", "expert"), split_axis=0, concat_axis=0, tiled=True)
    returned_flat = returned.reshape(slot_span, col_width)
    picked = jnp.take(returned_flat, destination.reshape(-1), axis=0).reshape(
        group_rows, top_count, col_width
    )
    expert_mix = jnp.sum(picked.astype(jnp.float32) * route_weights[:, :, None], axis=1).astype(
        jnp.bfloat16
    )
    return (attended, expert_mix)


def solution(mesh):
    return jax.shard_map(
        shards,
        mesh=mesh,
        in_specs=(
            P(("pool", "expert"), None),
            P(("pool", "expert"), None, None),
            P(("pool", "expert"), None),
            P(("pool", "expert")),
            P("pool", "expert"),
            P(None, "expert"),
            P("expert"),
            P("pool", None),
            P("pool", None),
            P(("pool", "expert"), None, None),
            P(("pool", "expert"), None, None),
            P(("pool", "expert"), None, None),
        ),
        out_specs=(P("pool", "expert"), P("pool", "expert")),
        check_vma=False,
    )
```

profile of v0, /device:TPU:1, one launch (start us, length us, event | category | flops | bytes accessed | tf_op | source)
XLA Modules:
  0.0 468.8 jit_solution(13245670071848037565)
XLA Ops:
  16.5 2.5 copy.100
  19.0 4.3 copy.118
  23.3 241.4 %while.11 = (s32[]{:T(128)}, bf16[8,4,4096]{2,1,0:T(4,128)(2,1)}, s32[8,4]{1,0:T(8,128)S(1)}, bf16[8,4,4096]{2,1,0:T(4,128)(2,1)}, s32[8,4,8]{2,1,0:T(4,128)S(1)}, /*index=5*/bf16[32,65536]{1,0:T(8,128)(2,1)}, s32[]{:T(128)}) while((s32[]{:T(128)}, bf16[8,4,4096]{2,1,0:T(4,128)(2,1)}, s32[8,4]{1,0:T(8,128)S(1)}, ...), condition=%wide.region_3.4_spmd.clone, body=%wide.region_0.3_spmd.clone.sunk | while | flops 168251520 | bytes 38803220 | solution.py:72
  24.2 5.7 %fusion.106 = bf16[32,65536]{1,0:T(8,128)(2,1)} fusion(bf16[32,65536]{1,0:T(8,128)(2,1)} %get-tuple-element.146, s32[32]{0:T(128)S(1)} %eq.385), kind=kOutput, calls=%fused_computation.15.clone.1 | convolution fusion | flops 134218752 | bytes 8388736 | tf_op jit(solution)/shard_map/while/body/eval_jaxpr/dot_general | solution.py:54
  29.9 5.6 %reshape.229 = bf16[4,512,1024]{2,1,0:T(8,128)(2,1)} reshape(bf16[32,65536]{1,0:T(8,128)(2,1)} %fusion.106) | data formatting | bytes 8388608 | tf_op jit(solution)/shard_map/while/body/eval_jaxpr/reshape | solution.py:55
  35.5 4.5 fusion.107
  40.0 4.2 copy.134
  44.2 4.2 copy.135
  50.6 2.3 convolution_convert_fusion.2
  54.5 5.4 %fusion.106 = bf16[32,65536]{1,0:T(8,128)(2,1)} fusion(bf16[32,65536]{1,0:T(8,128)(2,1)} %get-tuple-element.146, s32[32]{0:T(128)S(1)} %eq.385), kind=kOutput, calls=%fused_computation.15.clone.1 | convolution fusion | flops 134218752 | bytes 8388736 | tf_op jit(solution)/shard_map/while/body/eval_jaxpr/dot_general | solution.py:54
  59.9 5.9 %reshape.229 = bf16[4,512,1024]{2,1,0:T(8,128)(2,1)} reshape(bf16[32,65536]{1,0:T(8,128)(2,1)} %fusion.106) | data formatting | bytes 8388608 | tf_op jit(solution)/shard_map/while/body/eval_jaxpr/reshape | solution.py:55
  65.8 4.7 fusion.107
  70.5 4.2 copy.134
  74.7 4.2 copy.135
  81.0 2.3 convolution_convert_fusion.2
  85.0 5.4 %fusion.106 = bf16[32,65536]{1,0:T(8,128)(2,1)} fusion(bf16[32,65536]{1,0:T(8,128)(2,1)} %get-tuple-element.146, s32[32]{0:T(128)S(1)} %eq.385), kind=kOutput, calls=%fused_computation.15.clone.1 | convolution fusion | flops 134218752 | bytes 8388736 | tf_op jit(solution)/shard_map/while/body/eval_jaxpr/dot_general | solution.py:54
  90.4 5.6 %reshape.229 = bf16[4,512,1024]{2,1,0:T(8,128)(2,1)} reshape(bf16[32,65536]{1,0:T(8,128)(2,1)} %fusion.106) | data formatting | bytes 8388608 | tf_op jit(solution)/shard_map/while/body/eval_jaxpr/reshape | solution.py:55
  96.1 4.5 fusion.107
  100.5 4.2 copy.134
  104.7 4.2 copy.135
  111.0 2.7 convolution_convert_fusion.2
  115.3 5.5 %fusion.106 = bf16[32,65536]{1,0:T(8,128)(2,1)} fusion(bf16[32,65536]{1,0:T(8,128)(2,1)} %get-tuple-element.146, s32[32]{0:T(128)S(1)} %eq.385), kind=kOutput, calls=%fused_computation.15.clone.1 | convolution fusion | flops 134218752 | bytes 8388736 | tf_op jit(solution)/shard_map/while/body/eval_jaxpr/dot_general | solution.py:54
  120.9 5.6 %reshape.229 = bf16[4,512,1024]{2,1,0:T(8,128)(2,1)} reshape(bf16[32,65536]{1,0:T(8,128)(2,1)} %fusion.106) | data formatting | bytes 8388608 | tf_op jit(solution)/shard_map/while/body/eval_jaxpr/reshape | solution.py:55
  126.5 4.9 %fusion.107 = (bf16[4,512,512]{2,1,0:T(8,128)(2,1)}, bf16[4,512,512]{2,1,0:T(8,128)(2,1)}) fusion(bf16[4,512,1024]{2,1,0:T(8,128)(2,1)} %reshape.229), kind=kLoop, calls=%fused_computation.95.clone.1 | loop fusion | bytes 8388608 | tf_op jit(solution)/shard_map/while/body/eval_jaxpr/slice | solution.py:56
  131.4 4.2 copy.134
  135.5 4.2 copy.135
  141.9 2.3 convolution_convert_fusion.2
  145.8 5.5 %fusion.106 = bf16[32,65536]{1,0:T(8,128)(2,1)} fusion(bf16[32,65536]{1,0:T(8,128)(2,1)} %get-tuple-element.146, s32[32]{0:T(128)S(1)} %eq.385), kind=kOutput, calls=%fused_computation.15.clone.1 | convolution fusion | flops 134218752 | bytes 8388736 | tf_op jit(solution)/shard_map/while/body/eval_jaxpr/dot_general | solution.py:54
  151.2 5.6 %reshape.229 = bf16[4,512,1024]{2,1,0:T(8,128)(2,1)} reshape(bf16[32,65536]{1,0:T(8,128)(2,1)} %fusion.106) | data formatting | bytes 8388608 | tf_op jit(solution)/shard_map/while/body/eval_jaxpr/reshape | solution.py:55
  156.9 4.5 fusion.107
  161.3 4.2 copy.134
  165.5 4.2 copy.135
  175.7 5.5 %fusion.106 = bf16[32,65536]{1,0:T(8,128)(2,1)} fusion(bf16[32,65536]{1,0:T(8,128)(2,1)} %get-tuple-element.146, s32[32]{0:T(128)S(1)} %eq.385), kind=kOutput, calls=%fused_computation.15.clone.1 | convolution fusion | flops 134218752 | bytes 8388736 | tf_op jit(solution)/shard_map/while/body/eval_jaxpr/dot_general | solution.py:54
  181.2 5.6 %reshape.229 = bf16[4,512,1024]{2,1,0:T(8,128)(2,1)} reshape(bf16[32,65536]{1,0:T(8,128)(2,1)} %fusion.106) | data formatting | bytes 8388608 | tf_op jit(solution)/shard_map/while/body/eval_jaxpr/reshape | solution.py:55
  186.8 4.5 fusion.107
  191.3 4.2 copy.134
  195.5 4.2 copy.135
  205.7 5.5 %fusion.106 = bf16[32,65536]{1,0:T(8,128)(2,1)} fusion(bf16[32,65536]{1,0:T(8,128)(2,1)} %get-tuple-element.146, s32[32]{0:T(128)S(1)} %eq.385), kind=kOutput, calls=%fused_computation.15.clone.1 | convolution fusion | flops 134218752 | bytes 8388736 | tf_op jit(solution)/shard_map/while/body/eval_jaxpr/dot_general | solution.py:54
  211.2 5.6 %reshape.229 = bf16[4,512,1024]{2,1,0:T(8,128)(2,1)} reshape(bf16[32,65536]{1,0:T(8,128)(2,1)} %fusion.106) | data formatting | bytes 8388608 | tf_op jit(solution)/shard_map/while/body/eval_jaxpr/reshape | solution.py:55
  216.8 4.5 fusion.107
  221.3 4.2 copy.134
  225.4 4.2 copy.135
  235.6 5.4 %fusion.106 = bf16[32,65536]{1,0:T(8,128)(2,1)} fusion(bf16[32,65536]{1,0:T(8,128)(2,1)} %get-tuple-element.146, s32[32]{0:T(128)S(1)} %eq.385), kind=kOutput, calls=%fused_computation.15.clone.1 | convolution fusion | flops 134218752 | bytes 8388736 | tf_op jit(solution)/shard_map/while/body/eval_jaxpr/dot_general | solution.py:54
  241.1 5.6 %reshape.229 = bf16[4,512,1024]{2,1,0:T(8,128)(2,1)} reshape(bf16[32,65536]{1,0:T(8,128)(2,1)} %fusion.106) | data formatting | bytes 8388608 | tf_op jit(solution)/shard_map/while/body/eval_jaxpr/reshape | solution.py:55
  246.7 4.5 fusion.107
  251.2 4.2 copy.134
  255.3 4.2 copy.135
  265.7 20.7 %copy.96 = bf16[2048,4096]{1,0:T(8,128)(2,1)} copy(bf16[2048,4096]{0,1:T(8,128)(2,1)} %bitcast.146) | data formatting | bytes 33554432 | tf_op jit(solution)/shard_map/dot_general | solution.py:84
  286.4 9.3 %fusion.76 = f32[32,16,128]{2,0,1:T(8,128)} fusion(bf16[32,4096,1]{1,0,2:T(8,128)(2,1)S(1)} %reshape.220, bf16[16,128,4096]{2,1,0:T(8,128)(2,1)} %bitcast.145), kind=kOutput, calls=%fused_computation.98 | convolution fusion | flops 536870912 | bytes 17301504 | tf_op jit(solution)/shard_map/dot_general | solution.py:84
  295.7 8.9 %all-to-all-start = ((f32[32,16,128]{2,0,1:T(8,128)}), f32[32,16,128]{2,0,1:T(8,128)S(1)}, u32[]{:S(2)}, u32[]{:S(2)}) async-start(f32[32,16,128]{2,0,1:T(8,128)} %fusion.76), calls=%async_computation | async-start | bytes 524288 | tf_op jit(solution)/shard_map/all_to_all | solution.py:89
  304.6 2.5 fusion.50
  309.0 4.3 all-to-all-done
  315.5 4.4 all-to-all-start.1
  320.0 7.1 %all-to-all-done.1 = f32[16,1,512]{2,1,0:T(1,128)S(1)} async-done(((f32[16,1,512]{2,1,0:T(1,128)}), f32[16,1,512]{2,1,0:T(1,128)S(1)}, u32[]{:S(2)}, u32[]{:S(2)}) %all-to-all-start.1) | async-done | bytes 32800 | tf_op jit(solution)/shard_map/all_to_all | solution.py:14
  327.2 29.7 %fusion.23 = bf16[8192,128]{1,0:T(8,128)(2,1)} fusion(s32[512]{0:T(512)S(1)} %bitcast.162, s32[512]{0:T(512)S(1)} %bitcast.161, s32[512]{0:T(512)S(1)} %bitcast.160, s32[512]{0:T(512)S(1)} %bitcast.156, s32[512]{0:T(512)S(1)} %bitcast.157, s32[512]{0:T(512)S(1)} %bitcast.158, s32[512]{0:T(512)S(1)} %bitcast.159, s32[512]{0:T(512)S(1)} %bitcast.155, ...), kind=kOutput, calls=%fused_computation.39 | convolution fusion | flops 1208221696 | bytes 2247168 | tf_op jit(solution)/shard_map/dot_general | solution.py:119
  356.8 5.5 %all-to-all-start.2 = ((bf16[128,64,1,128]{3,1,2,0:T(8,128)(2,1)}), bf16[128,64,1,128]{3,1,2,0:T(8,128)(2,1)}, u32[]{:S(2)}, u32[]{:S(2)}) async-start(bf16[128,64,1,128]{3,1,2,0:T(8,128)(2,1)} %bitcast.151), calls=%async_computation.2 | async-start | bytes 4194304 | tf_op jit(solution)/shard_map/all_to_all | solution.py:125
  362.3 4.6 copy.119
  366.9 24.7 %all-to-all-done.2 = bf16[128,64,1,128]{3,1,2,0:T(8,128)(2,1)} async-done(((bf16[128,64,1,128]{3,1,2,0:T(8,128)(2,1)}), bf16[128,64,1,128]{3,1,2,0:T(8,128)(2,1)}, u32[]{:S(2)}, u32[]{:S(2)}) %all-to-all-start.2) | async-done | bytes 2097184 | tf_op jit(solution)/shard_map/all_to_all | solution.py:125
  391.6 5.5 %fusion.77 = f32[8,64,768,1]{2,1,3,0:T(8,128)} fusion(bf16[8,16,64,128]{3,2,1,0:T(8,128)(2,1)} %bitcast.18, bf16[16,128,768,1]{2,1,0,3:T(8,128)(2,1)} %bitcast.163), kind=kOutput, calls=%fused_computation.99 | convolution fusion | flops 1610612736 | bytes 6815744 | tf_op jit(solution)/shard_map/peixc,xecf->xpif/dot_general | solution.py:134
  397.2 8.4 %fusion.53 = bf16[8,64,16,128]{3,1,2,0:T(8,128)(2,1)} fusion(bf16[768,16,128]{2,1,0:T(8,128)(2,1)} %bitcast.149, bf16[8,16,64,128]{3,2,1,0:T(8,128)(2,1)} %bitcast.18, bf16[16,128,768,1]{2,1,0,3:T(8,128)(2,1)S(1)} %bitcast.141, f32[8,64,768,1]{2,1,3,0:T(8,128)} %fusion.77), kind=kOutput, calls=%fused_computation.65 | convolution fusion | flops 3224633344 | bytes 12058624 | tf_op jit(solution)/shard_map/xpif,xfec->peixc/dot_general | solution.py:140
  405.5 6.0 %all-to-all-start.3 = ((bf16[128,64,1,128]{3,1,2,0:T(8,128)(2,1)}), bf16[128,64,1,128]{3,1,2,0:T(8,128)(2,1)}, u32[]{:S(2)}, u32[]{:S(2)}) async-start(bf16[128,64,1,128]{3,1,2,0:T(8,128)(2,1)} %bitcast.150), calls=%async_computation.3 | async-start | bytes 4194304 | tf_op jit(solution)/shard_map/all_to_all | solution.py:144
  412.2 28.7 %all-to-all-done.3 = bf16[128,64,1,128]{3,1,2,0:T(8,128)(2,1)} async-done(((bf16[128,64,1,128]{3,1,2,0:T(8,128)(2,1)}), bf16[128,64,1,128]{3,1,2,0:T(8,128)(2,1)}, u32[]{:S(2)}, u32[]{:S(2)}) %all-to-all-start.3) | async-done | bytes 2097184 | tf_op jit(solution)/shard_map/all_to_all | solution.py:144
  440.9 16.1 %gather_fusion = bf16[4096,128]{1,0:T(8,128)(2,1)} fusion(bf16[8192,128]{1,0:T(8,128)(2,1)} %bitcast.35, s32[4096]{0:T(1024)S(1)} %broadcast_clamp_fusion), kind=kCustom, calls=%fused_computation | custom fusion | bytes 2113536 | tf_op jit(solution)/shard_map/jit(_take)/gather | solution.py:146
  457.0 4.7 %multiply_reduce_fusion = bf16[512,128]{1,0:T(8,128)(2,1)} fusion(bf16[4096,128]{1,0:T(8,128)(2,1)} %gather_fusion, f32[512,8]{1,0:T(8,128)S(1)} %copy.108, pred[512,8]{1,0:T(8,128)(4,1)S(1)} %copy.102), kind=kLoop, calls=%fused_computation.60 | loop fusion | flops 2031616 | bytes 1200128 | tf_op jit(solution)/shard_map/reduce_sum | solution.py:149
  (120 shorter events, 54.6 us)
Async XLA Ops:
  7.2 390.0 %copy-start = (bf16[1,2048,768]{2,1,0:T(8,128)(2,1)S(1)}, bf16[1,2048,768]{2,1,0:T(8,128)(2,1)}, u32[]{:S(2)}) copy-start(bf16[1,2048,768]{2,1,0:T(8,128)(2,1)} %param.24) | copy-start | bytes 9437188
  7.2 258.5 %all-gather.2.cloned.1.call-start = ((), (), s32[]{:S(2)}) async-start(), calls=%async_computation.4 | async-start | bytes 17825792 | tf_op jit(solution)/shard_map/all_gather | solution.py:86
  13.2 1.4 copy-start.1
  16.5 2.5 copy-start.2
  295.7 13.3 %copy-start.3 = (s32[512,8]{0,1:T(8,128)S(1)}, s32[512,8]{0,1:T(8,128)}, u32[]{:S(2)}) copy-start(s32[512,8]{0,1:T(8,128)} %param.21) | copy-start | bytes 49156
  295.7 31.5 %copy-start.5 = (f32[128]{0:T(128)S(1)}, f32[128]{0:T(128)}, u32[]{:S(2)}) copy-start(f32[128]{0:T(128)} %param.20) | copy-start | bytes 1540
  295.7 17.6 %all-to-all-start = ((f32[32,16,128]{2,0,1:T(8,128)}), f32[32,16,128]{2,0,1:T(8,128)S(1)}, u32[]{:S(2)}, u32[]{:S(2)}) async-start(f32[32,16,128]{2,0,1:T(8,128)} %fusion.76), calls=%async_computation | async-start | bytes 524288 | tf_op jit(solution)/shard_map/all_to_all | solution.py:89
  315.5 11.6 %all-to-all-start.1 = ((f32[16,1,512]{2,1,0:T(1,128)}), f32[16,1,512]{2,1,0:T(1,128)S(1)}, u32[]{:S(2)}, u32[]{:S(2)}) async-start(f32[16,1,512]{2,1,0:T(1,128)} %broadcast_in_dim.35), calls=%async_computation.1 | async-start | bytes 65536 | tf_op jit(solution)/shard_map/all_to_all | solution.py:14
  356.8 34.8 %all-to-all-start.2 = ((bf16[128,64,1,128]{3,1,2,0:T(8,128)(2,1)}), bf16[128,64,1,128]{3,1,2,0:T(8,128)(2,1)}, u32[]{:S(2)}, u32[]{:S(2)}) async-start(bf16[128,64,1,128]{3,1,2,0:T(8,128)(2,1)} %bitcast.151), calls=%async_computation.2 | async-start | bytes 4194304 | tf_op jit(solution)/shard_map/all_to_all | solution.py:125
  405.5 6.3 %copy-start.4 = (f32[512,8]{0,1:T(8,128)S(1)}, f32[512,8]{0,1:T(8,128)}, u32[]{:S(2)}) copy-start(f32[512,8]{0,1:T(8,128)} %param.22) | copy-start | bytes 49156
  405.5 35.4 %all-to-all-start.3 = ((bf16[128,64,1,128]{3,1,2,0:T(8,128)(2,1)}), bf16[128,64,1,128]{3,1,2,0:T(8,128)(2,1)}, u32[]{:S(2)}, u32[]{:S(2)}) async-start(bf16[128,64,1,128]{3,1,2,0:T(8,128)(2,1)} %bitcast.150), calls=%async_computation.3 | async-start | bytes 4194304 | tf_op jit(solution)/shard_map/all_to_all | solution.py:144
Sparse Core Ops, SparseCore 0:
  10.3 121.9 all-gather.1
where the time goes:
time: 477 us; the launch traced here: 469 us
  local copies, waits for them, and re-layouts  219 us (46%)
  matrix products  131 us (27%)
  waiting for transfers between devices  65.5 us (14%)
  starting transfers between devices  24.9 us (5%)
  between operations  14.4 us (3%)
  other arithmetic  13.7 us (3%)
    while x24, local copies, waits for them, and re-layouts  72.8 us
    reshape x8, local copies, waits for them, and re-layouts, attend(): gathered = gathered.reshape(step_rows, context, kv_width)  45.3 us
    dot_general x8, matrix products, attend(): gathered = jnp.dot(selector, kv_flat, preferred_element_type=jnp.bfloat16)  43.9 us
    slice x8, local copies, waits for them, and re-layouts, attend(): gathered[:, :, :kv_half].reshape(step_rows, context, kv_heads, HEAD_DIM)  36.3 us
    dot_general x1, matrix products, shards(): lax.dot_general(chosen, normed, (((0,), (0,)), ((), ())), preferred_eleme...  29.7 us
    all_to_all x1, waiting for transfers between devices, shards(): lax.all_to_all(result, ('pool', 'expert'), split_axis=0, concat_axis=0, t...  28.7 us
    all_to_all x1, waiting for transfers between devices, shards(): lax.all_to_all(outgoing.reshape(device_count, capacity, local_count, col_...  24.7 us
    dot_general x1, local copies, waits for them, and re-layouts, shards(): jnp.dot(attention, lax.all_gather(out_weight, 'expert', axis=1, tiled=Tru...  20.7 us
  transfers between devices with their start and end apart: 5, of which 4 were waited for; matrix products, arithmetic and copies ran while one was open for 57% of the time, Pallas kernels for 0%

commit v1 on v0

v1 whole, which is shorter than its diff:
```python
import math

import jax
import jax.numpy as jnp
from jax import lax
from jax.experimental import pallas as pl
from jax.experimental.pallas import tpu as pltpu
from jax.sharding import PartitionSpec as P

HD = 128
EPS = 1e-06
MESH = pl.DeviceIdType.MESH
F32 = jnp.float32
BF16 = jnp.bfloat16
VM = pl.BlockSpec(memory_space=pltpu.VMEM)
ANY = pl.BlockSpec(memory_space=pl.ANY)
NT = (((1,), (1,)), ((), ()))
TN = (((0,), (0,)), ((), ()))


def attend_project(
    q_ref,
    kv_hbm,
    bi_ref,
    len_ref,
    res_ref,
    w_hbm,
    gain_ref,
    att_ref,
    gall_ref,
    kv,
    wown,
    wsib,
    ressib,
    gath,
    s_scr,
    p_scr,
    linv,
    bias,
    stage,
    acc,
    in_sem,
    w_sem,
    y_s,
    y_r,
    z_s,
    z_r,
    sib_s,
    sib_r,
    gain_s,
    gain_r,
):
    e = lax.axis_index("expert")
    core = e % 2
    chip = e // 2
    y_hi = chip // 4
    z = chip % 4
    sib = e + 1 - 2 * core
    chip_y = chip + 4 - 8 * y_hi
    z_up = (z + 1) % 4
    z_dn = (z + 3) % 4
    z_op = (z + 2) % 4
    chip_up = y_hi * 4 + z_up
    chip_dn = y_hi * 4 + z_dn
    chip_op = y_hi * 4 + z_op
    flip = 4 - 8 * y_hi
    dev_y = chip_y * 2 + core
    dev_up = chip_up * 2 + core
    dev_dn = chip_dn * 2 + core

    barrier = pltpu.get_barrier_semaphore()
    for d in range(1, 16):
        pl.semaphore_signal(barrier, inc=1, device_id={"expert": (e + d) % 16}, device_id_type=MESH)

    def fetch(i):
        return pltpu.make_async_copy(kv_hbm.at[:, pl.ds(i * HD, HD)], kv.at[i], in_sem.at[i])

    fetch_w = pltpu.make_async_copy(w_hbm, wown, w_sem)
    for g in range(4):
        fetch(g).start()
        fetch(4 + g).start()
    fetch_w.start()

    rows, span = bias.shape
    lane = lax.broadcasted_iota(jnp.int32, (rows, span), 1)
    block = lane // 64
    offset = lane % 64
    count = jnp.zeros((rows, span), F32)
    for j in range(8):
        live = (block == bi_ref[:, j : j + 1]) & (offset < len_ref[...] - 64 * j)
        count = count + jnp.where(live, 1.0, 0.0)
    bias[...] = jnp.where(count > 0.0, jnp.log2(jnp.maximum(count, 1.0)), -1e30)

    factor = HD ** (-0.5) * math.log2(math.e)

    def attend(g):
        fetch(g).wait()
        query = jnp.concatenate(
            [q_ref[:, (g * 8 + i) * HD : (g * 8 + i + 1) * HD] for i in range(8)], axis=0
        )
        s_scr[...] = lax.dot_general(query, kv[g], NT, preferred_element_type=F32)

        def soften(r, carry):
            at = pl.ds(pl.multiple_of(r * 16, 16), 16)
            of = pl.ds(pl.multiple_of((r % 2) * 16, 16), 16)
            x = s_scr[at, :] * factor + bias[of, :]
            top = jnp.max(x, axis=1, keepdims=True)
            ex = jnp.exp2(x - top)
            total = jnp.sum(ex, axis=1, keepdims=True)
            p_scr[at, :] = ex.astype(BF16)
            linv[at, :] = jnp.broadcast_to(1.0 / total, (16, HD))
            return carry

        lax.fori_loop(0, 16, soften, 0)
        fetch(4 + g).wait()
        o = jnp.dot(p_scr[...], kv[4 + g], preferred_element_type=F32) * linv[...]
        o = o.astype(BF16)
        for i in range(8):
            gath[chip, g, :, i * HD : (i + 1) * HD] = o[i * 32 : (i + 1) * 32]

    def remote(src, dst, ssem, rsem, dev):
        return pltpu.make_async_remote_copy(
            src_ref=src,
            dst_ref=dst,
            send_sem=ssem,
            recv_sem=rsem,
            device_id={"expert": dev},
            device_id_type=MESH,
        )

    lo, hi = pl.ds(0, 16), pl.ds(16, 16)

    def block_copy(c, g, ssem, rsem, dev, part=None):
        ref = gath.at[c, g] if part is None else gath.at[c, g, part]
        return remote(ref, ref, ssem, rsem, dev)

    def own_y(g):
        return block_copy(chip, g, y_s.at[g], y_r.at[g], dev_y)

    def z_copy(kind, g, way):
        dev = dev_up if way == 0 else dev_dn
        ss, rs = z_s.at[kind, g, way], z_r.at[kind, g, way]
        if kind == 0:
            return block_copy(chip, g, ss, rs, dev)
        if kind == 1:
            return block_copy(chip_y, g, ss, rs, dev)
        source = chip_dn if way == 0 else chip_up
        if kind == 3:
            source = source + flip
        return block_copy(source, g, ss, rs, dev, lo if way == 0 else hi)

    def send_own(g):
        z_copy(0, g, 0).start()
        z_copy(0, g, 1).start()
        own_y(g).start()

    def send_partner(g):
        own_y(g).wait_recv()
        z_copy(1, g, 0).start()
        z_copy(1, g, 1).start()

    def relay(kind, g):
        for way in (0, 1):
            z_copy(kind, g, way).wait_recv()
            z_copy(kind + 2, g, way).start()

    def finish(g):
        for way in (0, 1):
            z_copy(2, g, way).wait_recv()
            z_copy(3, g, way).wait_recv()

    def project(g):
        depth = 8 * HD
        at = pl.ds(g * depth, depth)
        rows_g = gath[:, g].reshape(256, depth)
        part = jnp.dot(rows_g, wown[at, :], preferred_element_type=F32)
        other = jnp.dot(rows_g, wsib[at, :], preferred_element_type=F32)
        if g == 0:
            acc[0] = part
            acc[1] = other
        else:
            acc[0] += part
            acc[1] += other

    attend(0)
    pl.semaphore_wait(barrier, 15)
    send_own(0)
    send_w = remote(w_hbm, wsib, sib_s.at[0], sib_r.at[0], sib)
    send_w.start()
    send_res = remote(res_ref.at[:, 1 - core], ressib, sib_s.at[1], sib_r.at[1], sib)
    send_res.start()
    gall_ref[e] = gain_ref[...]
    gains = [
        remote(gain_ref, gall_ref.at[e], gain_s.at[d], gain_r.at[d], (e + d) % 16)
        for d in range(1, 16)
    ]
    for gain in gains:
        gain.start()
    attend(1)
    send_own(1)
    send_partner(0)
    relay(0, 0)
    attend(2)
    send_own(2)
    relay(1, 0)
    send_partner(1)
    relay(0, 1)
    attend(3)
    send_own(3)
    relay(1, 1)
    send_partner(2)
    relay(0, 2)
    fetch_w.wait()
    send_w.wait_recv()
    finish(0)
    project(0)
    relay(1, 2)
    send_partner(3)
    relay(0, 3)
    finish(1)
    project(1)
    relay(1, 3)
    finish(2)
    project(2)
    finish(3)
    project(3)
    send_res.wait_recv()
    stage[...] = (ressib[...].astype(F32) + acc[1].reshape(8, 32, HD)).astype(BF16)
    send_out = remote(stage, att_ref.at[:, core], sib_s.at[2], sib_r.at[2], sib)
    send_out.start()
    att_ref[:, core] = (res_ref[:, core].astype(F32) + acc[0].reshape(8, 32, HD)).astype(BF16)
    for g in range(4):
        own_y(g).wait_send()
        for kind in range(4):
            z_copy(kind, g, 0).wait_send()
            z_copy(kind, g, 1).wait_send()
    send_w.wait_send()
    send_res.wait_send()
    for gain in gains:
        gain.wait()
    send_out.wait()


def attention_stage(queries, kv_cache, block_index, lengths, residual, out_weight, norm_gain):
    rows = queries.shape[0]
    span = kv_cache.shape[0] * kv_cache.shape[1]
    width = kv_cache.shape[2]
    dma = pltpu.SemaphoreType.DMA
    att, gall = pl.pallas_call(
        attend_project,
        out_shape=(
            jax.ShapeDtypeStruct((8, 2, 32, HD), BF16),
            jax.ShapeDtypeStruct((16, 1, HD), F32),
        ),
        in_specs=[VM, ANY, VM, VM, VM, ANY, VM],
        out_specs=(VM, VM),
        scratch_shapes=[
            pltpu.VMEM((width // HD, span, HD), BF16),
            pltpu.VMEM(out_weight.shape, BF16),
            pltpu.VMEM(out_weight.shape, BF16),
            pltpu.VMEM((8, 32, HD), BF16),
            pltpu.VMEM((8, 4, 32, 8 * HD), BF16),
            pltpu.VMEM((256, span), F32),
            pltpu.VMEM((256, span), BF16),
            pltpu.VMEM((256, HD), F32),
            pltpu.VMEM((rows, span), F32),
            pltpu.VMEM((8, 32, HD), BF16),
            pltpu.VMEM((2, 256, HD), F32),
            dma((8,)),
            dma,
            dma((4,)),
            dma((4,)),
            dma((4, 4, 2)),
            dma((4, 4, 2)),
            dma((3,)),
            dma((3,)),
            dma((16,)),
            dma((16,)),
        ],
        compiler_params=pltpu.CompilerParams(
            collective_id=0, has_side_effects=True, vmem_limit_bytes=60 * 1024 * 1024
        ),
        name="attend_project",
    )(
        queries,
        kv_cache.reshape(span, width),
        block_index,
        lengths.reshape(rows, 1),
        residual.reshape(8, 2, 32, HD),
        out_weight,
        norm_gain.reshape(1, HD),
    )
    return att.reshape(512, HD), gall.reshape(1, 16 * HD)


def dispatch(ids_ref, rw_ref, x_ref, out_ref, slot_ref, wt_ref):
    experts, rows = slot_ref.shape
    which = lax.broadcasted_iota(jnp.int32, (experts, rows), 0)
    named = jnp.zeros((experts, rows), F32)
    weight = jnp.zeros((experts, rows), F32)
    for k in range(8):
        same = which == ids_ref[k : k + 1, :]
        named = named + jnp.where(same, 1.0, 0.0)
        weight = weight + jnp.where(same, rw_ref[k : k + 1, :], 0.0)
    wt_ref[...] = weight
    early = lax.broadcasted_iota(jnp.int32, (rows, rows), 0)
    late = lax.broadcasted_iota(jnp.int32, (rows, rows), 1)
    ahead = jnp.where(early < late, 1.0, 0.0).astype(BF16)
    slot = jnp.dot(named.astype(BF16), ahead, preferred_element_type=F32)
    slot_ref[...] = jnp.where(named > 0.0, slot, -1.0)
    place = lax.broadcasted_iota(jnp.int32, (64, rows), 0).astype(F32)

    def some(i, carry):
        parts = [
            jnp.where(slot_ref[pl.ds(i * 4 + u, 1), :] == place, 1.0, 0.0).astype(BF16)
            for u in range(4)
        ]
        chosen = jnp.concatenate(parts, axis=0)
        out_ref[pl.ds(pl.multiple_of(i * 256, 256), 256), :] = jnp.dot(
            chosen, x_ref[...], preferred_element_type=F32
        ).astype(BF16)
        return carry

    lax.fori_loop(0, experts // 4, some, 0)


def expert_rows(x_ref, gain_ref, g_hbm, u_hbm, d_hbm, y_ref, gw, uw, dw, xs, hid, sem):
    copies = [
        pltpu.make_async_copy(g_hbm.at[0], gw, sem.at[0]),
        pltpu.make_async_copy(u_hbm.at[0], uw, sem.at[1]),
        pltpu.make_async_copy(d_hbm.at[0], dw, sem.at[2]),
    ]
    for copy in copies:
        copy.start()

    def norm(i, carry):
        p = i // 4
        at = pl.ds(pl.multiple_of((i % 4) * 16, 16), 16)
        x = jnp.concatenate([x_ref[p, f, at, :] for f in range(16)], axis=1).astype(F32)
        inv = lax.rsqrt(jnp.sum(x * x, axis=1, keepdims=True) / (16 * HD) + EPS)
        xs[pl.ds(pl.multiple_of(i * 16, 16), 16), :] = (x * inv * gain_ref[...]).astype(BF16)
        return carry

    lax.fori_loop(0, 32, norm, 0)
    copies[0].wait()
    copies[1].wait()

    def up(i, carry):
        at = pl.ds(pl.multiple_of(i * 256, 256), 256)
        gate = jnp.dot(xs[...], gw[:, at], preferred_element_type=F32)
        upper = jnp.dot(xs[...], uw[:, at], preferred_element_type=F32)
        hid[:, at] = (gate / (1.0 + jnp.exp(-gate)) * upper).astype(BF16)
        return carry

    lax.fori_loop(0, 3, up, 0)
    copies[2].wait()

    def down(i, carry):
        at = pl.ds(pl.multiple_of(i * 256, 256), 256)
        y = jnp.dot(hid[...], dw[:, at], preferred_element_type=F32).astype(BF16)
        for p in range(8):
            for h in range(2):
                y_ref[p, i * 2 + h] = y[p * 64 : (p + 1) * 64, h * HD : (h + 1) * HD]
        return carry

    lax.fori_loop(0, 8, down, 0)


def combine(slot_ref, wt_ref, y_ref, out_ref, acc):
    experts, rows = slot_ref.shape
    place = lax.broadcasted_iota(jnp.int32, (64, rows), 0).astype(F32)
    acc[...] = jnp.zeros_like(acc)

    def some(i, carry):
        parts = [
            jnp.where(
                slot_ref[pl.ds(i * 4 + u, 1), :] == place, wt_ref[pl.ds(i * 4 + u, 1), :], 0.0
            ).astype(BF16)
            for u in range(4)
        ]
        chosen = jnp.concatenate(parts, axis=0)
        y = y_ref[pl.ds(pl.multiple_of(i * 256, 256), 256), :]
        acc[...] += lax.dot_general(y, chosen, TN, preferred_element_type=F32)
        return carry

    lax.fori_loop(0, experts // 4, some, 0)
    out_ref[...] = acc[...].T.astype(BF16)


def shards(
    queries,
    kv_cache,
    block_index,
    lengths,
    residual,
    out_weight,
    norm_gain,
    expert_ids,
    route_weights,
    gate_weight,
    up_weight,
    down_weight,
):
    attended, gain = attention_stage(
        queries, kv_cache, block_index, lengths, residual, out_weight, norm_gain
    )
    big = pltpu.CompilerParams(vmem_limit_bytes=56 * 1024 * 1024)
    outgoing, slot, wt = pl.pallas_call(
        dispatch,
        out_shape=(
            jax.ShapeDtypeStruct((128 * 64, HD), BF16),
            jax.ShapeDtypeStruct((128, 512), F32),
            jax.ShapeDtypeStruct((128, 512), F32),
        ),
        in_specs=[VM] * 3,
        out_specs=(VM, VM, VM),
        compiler_params=big,
        name="dispatch",
    )(expert_ids.T, route_weights.T, attended)
    axes = ("pool", "expert")
    received = lax.all_to_all(outgoing.reshape(128, 64, HD), axes, 0, 0, tiled=True)
    width, hidden = gate_weight.shape[1:]
    result = pl.pallas_call(
        expert_rows,
        out_shape=jax.ShapeDtypeStruct((8, 16, 64, HD), BF16),
        in_specs=[VM, VM, ANY, ANY, ANY],
        out_specs=VM,
        scratch_shapes=[
            pltpu.VMEM((width, hidden), BF16),
            pltpu.VMEM((width, hidden), BF16),
            pltpu.VMEM((hidden, width), BF16),
            pltpu.VMEM((512, width), BF16),
            pltpu.VMEM((512, hidden), BF16),
            pltpu.SemaphoreType.DMA((3,)),
        ],
        compiler_params=big,
        name="expert_rows",
    )(received.reshape(8, 16, 64, HD), gain, gate_weight, up_weight, down_weight)
    returned = lax.all_to_all(result.reshape(128, 64, HD), axes, 0, 0, tiled=True)
    mixed = pl.pallas_call(
        combine,
        out_shape=jax.ShapeDtypeStruct((512, HD), BF16),
        in_specs=[VM] * 3,
        out_specs=VM,
        scratch_shapes=[pltpu.VMEM((HD, 512), F32)],
        compiler_params=big,
        name="combine",
    )(slot, wt, returned.reshape(128 * 64, HD))
    return (attended, mixed)


def solution(mesh):
    return jax.shard_map(
        shards,
        mesh=mesh,
        in_specs=(
            P(("pool", "expert"), None),
            P(("pool", "expert"), None, None),
            P(("pool", "expert"), None),
            P(("pool", "expert")),
            P("pool", "expert"),
            P(None, "expert"),
            P("expert"),
            P("pool", None),
            P("pool", None),
            P(("pool", "expert"), None, None),
            P(("pool", "expert"), None, None),
            P(("pool", "expert"), None, None),
        ),
        out_specs=(P("pool", "expert"), P("pool", "expert")),
        check_vma=False,
    )
```

time: 477 us -> 150 us (0.31); the launches traced: 469 us -> 150 us
  local copies, waits for them, and re-layouts: 219 us -> 3.37 us
  matrix products: 131 us -> 0 us
  blocking collectives: 0 us -> 73.5 us
  Pallas kernels: 0 us -> 72.3 us
  waiting for transfers between devices: 65.5 us -> 0 us
  starting transfers between devices: 24.9 us -> 0 us
  between operations: 14.4 us -> 0.66 us
  other arithmetic: 13.7 us -> 0 us
    dot_general x28 -> x0, matrix products: 131 us -> none  [the longest x8 43.9 us: attend(): gathered = jnp.dot(selector, kv_flat, preferred_element_type=jnp.bfloat16)]
    all_to_all x0 -> x2, blocking collectives: none -> 73.5 us  [the longest x1 37.8 us: shards(): lax.all_to_all(outgoing.reshape(128, 64, HD), axes, 0, 0, tiled=True)]
    while x24 -> x0, local copies, waits for them, and re-layouts: 72.8 us -> none
    pallas_call x0 -> x4, Pallas kernels: none -> 72.3 us  [the longest x1 39.6 us: attention_stage(): pl.pallas_call(attend_project, out_shape=(jax.ShapeDtypeStruct((8, 2, 32,...]
    all_to_all x4 -> x0, waiting for transfers between devices: 64.8 us -> none  [the longest x1 28.7 us: shards(): lax.all_to_all(result, ('pool', 'expert'), split_axis=0, concat_axis=0, t...]
    reshape x12 -> x1, local copies, waits for them, and re-layouts: 48.9 us -> 1.34 us  [attention_stage(): lengths.reshape(rows, 1)]
    slice x9 -> x0, local copies, waits for them, and re-layouts: 36.3 us -> none  [the longest x8 36.3 us: attend(): gathered[:, :, :kv_half].reshape(step_rows, context, kv_heads, HEAD_DIM)]
    all_to_all x4 -> x0, starting transfers between devices: 24.8 us -> none  [the longest x1 8.91 us: shards(): lax.all_to_all(proj_rows, 'expert', split_axis=1, concat_axis=0, tiled=True)]
  transfers between devices with their start and end apart: 5 -> 0, of which waited for: 4 -> 0; matrix products, arithmetic and copies ran while one was open for 57% -> 0% of each run, Pallas kernels for 0% -> 0%
where the time goes in v1:
time: 150 us
  blocking collectives  73.5 us (49%)
  Pallas kernels  72.3 us (48%)
  local copies, waits for them, and re-layouts  3.37 us (2%)
    pallas_call x1, Pallas kernels, attention_stage(): pl.pallas_call(attend_project, out_shape=(jax.ShapeDtypeStruct((8, 2, 32,...  39.6 us
    all_to_all x1, blocking collectives, shards(): lax.all_to_all(outgoing.reshape(128, 64, HD), axes, 0, 0, tiled=True)  37.8 us
    all_to_all x1, blocking collectives, shards(): lax.all_to_all(result.reshape(128, 64, HD), axes, 0, 0, tiled=True)  35.7 us
    pallas_call x1, Pallas kernels, shards(): pl.pallas_call(expert_rows, out_shape=jax.ShapeDtypeStruct((8, 16, 64, HD...  13.6 us
    pallas_call x1, Pallas kernels, shards(): pl.pallas_call(dispatch, out_shape=(jax.ShapeDtypeStruct((128 * 64, HD),...  9.74 us
    pallas_call x1, Pallas kernels, shards(): pl.pallas_call(combine, out_shape=jax.ShapeDtypeStruct((512, HD), BF16),...  9.32 us

profile of v1, /device:TPU:1, one launch (start us, length us, event | category | flops | bytes accessed | tf_op | source)
XLA Modules:
  0.0 149.8 jit_solution(11493550428309390227)
XLA Ops:
  0.6 1.4 copy.14.bi_ref
  2.0 1.3 copy.15.len_ref
  3.3 39.6 %attend_project.1 = (bf16[8,2,32,128]{3,2,1,0:T(8,128)(2,1)}, f32[16,1,128]{2,1,0:T(1,128)}) custom-call(bf16[32,4096]{1,0:T(8,128)(2,1)} %q_ref.1, bf16[2048,1024]{1,0:T(8,128)(2,1)} %bitcast.15, s32[32,8]{1,0:T(8,128)} %copy.14.bi_ref, s32[32,1]{1,0:T(8,128)} %copy.15.len_ref, bf16[8,2,32,128]{3,2,1,0:T(8,128)(2,1)} %bitcast.19, bf16[4096,128]{1,0:T(8,128)(2,1)} %w_hbm.1, ...), custom_call_target="tpu_custom_call" | custom-call | tf_op jit(solution)/shard_map/attend_project/pallas_call | solution.py:249
  43.0 9.7 %dispatch.1 = (bf16[8192,128]{1,0:T(8,128)(2,1)}, f32[128,512]{1,0:T(8,128)}, f32[128,512]{1,0:T(8,128)}) custom-call(s32[8,512]{1,0:T(8,128)} %bitcast.20, f32[8,512]{1,0:T(8,128)} %bitcast.21, bf16[512,128]{1,0:T(8,128)(2,1)} %bitcast.17), custom_call_target="tpu_custom_call" | custom-call | tf_op jit(solution)/shard_map/dispatch/pallas_call | solution.py:408
  52.7 37.8 %all_to_all.10 = bf16[128,64,128]{2,1,0:T(8,128)(2,1)} all-to-all(bf16[128,64,128]{2,1,0:T(8,128)(2,1)} %bitcast.16), channel_id=1, replica_groups=mesh['pool'=8,'expert'=16] {'pool','expert'}, dimensions={0} | all-to-all | bytes 4194304 | tf_op jit(solution)/shard_map/all_to_all | solution.py:421
  90.5 13.6 %expert_rows.1 = bf16[8,16,64,128]{3,2,1,0:T(8,128)(2,1)} custom-call(bf16[8,16,64,128]{3,2,1,0:T(8,128)(2,1)} %bitcast.13, f32[1,2048]{1,0:T(1,128)} %bitcast.22, bf16[1,2048,768]{2,1,0:T(8,128)(2,1)} %g_hbm.1, bf16[1,2048,768]{2,1,0:T(8,128)(2,1)} %u_hbm.1, bf16[1,768,2048]{2,1,0:T(8,128)(2,1)} %d_hbm.1), custom_call_target="tpu_custom_call" | custom-call | tf_op jit(solution)/shard_map/expert_rows/pallas_call | solution.py:423
  104.1 0.0 copy-start
  104.2 35.7 %all_to_all.11 = bf16[128,64,128]{2,1,0:T(8,128)(2,1)} all-to-all(bf16[128,64,128]{2,1,0:T(8,128)(2,1)} %bitcast.14), channel_id=1, replica_groups=mesh['pool'=8,'expert'=16] {'pool','expert'}, dimensions={0} | all-to-all | bytes 4194304 | tf_op jit(solution)/shard_map/all_to_all | solution.py:439
  139.8 9.3 %combine.1 = bf16[512,128]{1,0:T(8,128)(2,1)} custom-call(f32[128,512]{1,0:T(8,128)} %get-tuple-element.8.slot_ref, f32[128,512]{1,0:T(8,128)} %get-tuple-element.9.wt_ref, bf16[8192,128]{1,0:T(8,128)(2,1)} %bitcast.12), custom_call_target="tpu_custom_call" | custom-call | tf_op jit(solution)/shard_map/combine/pallas_call | solution.py:440
  149.1 0.0 copy-done
  149.1 0.7 copy.17
Async XLA Ops:
  104.1 45.0 %copy-start = (bf16[8,2,32,128]{3,2,1,0:T(8,128)(2,1)S(1)}, bf16[8,2,32,128]{3,2,1,0:T(8,128)(2,1)}, u32[]{:S(2)}) copy-start(bf16[8,2,32,128]{3,2,1,0:T(8,128)(2,1)} %get-tuple-element.7) | copy-start | bytes 393220

commit v2 on v1

v2 whole, which is shorter than its diff:
```python
import math

import jax
import jax.numpy as jnp
from jax import lax
from jax.experimental import pallas as pl
from jax.experimental.pallas import tpu as pltpu
from jax.sharding import PartitionSpec as P

HD = 128
EPS = 1e-06
MESH = pl.DeviceIdType.MESH
F32 = jnp.float32
BF16 = jnp.bfloat16
VM = pl.BlockSpec(memory_space=pltpu.VMEM)
ANY = pl.BlockSpec(memory_space=pl.ANY)
NT = (((1,), (1,)), ((), ()))
TN = (((0,), (0,)), ((), ()))
SLOTS = 64


def layer(
    q_ref,
    kv_hbm,
    bi_ref,
    len_ref,
    res_ref,
    w_hbm,
    gain_ref,
    ids_ref,
    rw_ref,
    g_hbm,
    u_hbm,
    d_hbm,
    att_ref,
    mix_ref,
    kv,
    wown,
    wsib,
    ressib,
    gath,
    s_scr,
    p_scr,
    linv,
    bias,
    stage,
    acc,
    table,
    gall_ref,
    slot_ref,
    wt_ref,
    gw,
    uw,
    dw,
    obuf,
    rbuf,
    ybuf,
    zbuf,
    xs,
    hid,
    mixt,
    in_sem,
    w_sem,
    y_s,
    y_r,
    z_s,
    z_r,
    sib_s,
    sib_r,
    gain_s,
    gain_r,
    ffn_sem,
    out_s,
    out_r,
    back_s,
    back_r,
):
    p = lax.axis_index("pool")
    e = lax.axis_index("expert")
    core = e % 2
    chip = e // 2
    y_hi = chip // 4
    z = chip % 4
    sib = e + 1 - 2 * core
    chip_y = chip + 4 - 8 * y_hi
    z_up = (z + 1) % 4
    z_dn = (z + 3) % 4
    z_op = (z + 2) % 4
    chip_up = y_hi * 4 + z_up
    chip_dn = y_hi * 4 + z_dn
    chip_op = y_hi * 4 + z_op
    flip = 4 - 8 * y_hi
    dev_y = chip_y * 2 + core
    dev_up = chip_up * 2 + core
    dev_dn = chip_dn * 2 + core

    me = p * 16 + e
    barrier = pltpu.get_barrier_semaphore()

    def fetch(i):
        return pltpu.make_async_copy(kv_hbm.at[:, pl.ds(i * HD, HD)], kv.at[i], in_sem.at[i])

    fetch_w = pltpu.make_async_copy(w_hbm, wown, w_sem)
    for g in range(4):
        fetch(g).start()
        fetch(4 + g).start()
    fetch_w.start()
    ffn = [
        pltpu.make_async_copy(g_hbm.at[0], gw, ffn_sem.at[0]),
        pltpu.make_async_copy(u_hbm.at[0], uw, ffn_sem.at[1]),
        pltpu.make_async_copy(d_hbm.at[0], dw, ffn_sem.at[2]),
    ]
    for copy in ffn:
        copy.start()

    def greet(d, carry):
        t = lax.rem(me + d, 128)
        pl.semaphore_signal(
            barrier,
            inc=1,
            device_id={"pool": lax.div(t, 16), "expert": lax.rem(t, 16)},
            device_id_type=MESH,
        )
        return carry

    lax.fori_loop(1, 128, greet, 0)

    rows, span = bias.shape
    lane = lax.broadcasted_iota(jnp.int32, (rows, span), 1)
    block = lane // 64
    offset = lane % 64
    count = jnp.zeros((rows, span), F32)
    table[...] = jnp.zeros_like(table)
    table[0:8, 0:rows] = bi_ref[...]
    table[8:16, 0:rows] = jnp.broadcast_to(len_ref[...], (8, rows))
    turned = table[...].T[0:rows, :]
    for j in range(8):
        live = (block == turned[:, j : j + 1]) & (offset < turned[:, 8:9] - 64 * j)
        count = count + jnp.where(live, 1.0, 0.0)
    bias[...] = jnp.where(count > 0.0, jnp.log2(jnp.maximum(count, 1.0)), -1e30)

    factor = HD ** (-0.5) * math.log2(math.e)

    def attend(g):
        fetch(g).wait()
        query = jnp.concatenate(
            [q_ref[:, (g * 8 + i) * HD : (g * 8 + i + 1) * HD] for i in range(8)], axis=0
        )
        s_scr[...] = lax.dot_general(query, kv[g], NT, preferred_element_type=F32)

        def soften(r, carry):
            at = pl.ds(pl.multiple_of(r * 16, 16), 16)
            of = pl.ds(pl.multiple_of((r % 2) * 16, 16), 16)
            x = s_scr[at, :] * factor + bias[of, :]
            top = jnp.max(x, axis=1, keepdims=True)
            ex = jnp.exp2(x - top)
            total = jnp.sum(ex, axis=1, keepdims=True)
            p_scr[at, :] = ex.astype(BF16)
            linv[at, :] = jnp.broadcast_to(1.0 / total, (16, HD))
            return carry

        lax.fori_loop(0, 16, soften, 0)
        fetch(4 + g).wait()
        o = jnp.dot(p_scr[...], kv[4 + g], preferred_element_type=F32) * linv[...]
        o = o.astype(BF16)
        for i in range(8):
            gath[chip, g, :, i * HD : (i + 1) * HD] = o[i * 32 : (i + 1) * 32]

    def remote(src, dst, ssem, rsem, dev):
        return pltpu.make_async_remote_copy(
            src_ref=src,
            dst_ref=dst,
            send_sem=ssem,
            recv_sem=rsem,
            device_id={"expert": dev},
            device_id_type=MESH,
        )

    lo, hi = pl.ds(0, 16), pl.ds(16, 16)

    def block_copy(c, g, ssem, rsem, dev, part=None):
        ref = gath.at[c, g] if part is None else gath.at[c, g, part]
        return remote(ref, ref, ssem, rsem, dev)

    def own_y(g):
        return block_copy(chip, g, y_s.at[g], y_r.at[g], dev_y)

    def z_copy(kind, g, way):
        dev = dev_up if way == 0 else dev_dn
        ss, rs = z_s.at[kind, g, way], z_r.at[kind, g, way]
        if kind == 0:
            return block_copy(chip, g, ss, rs, dev)
        if kind == 1:
            return block_copy(chip_y, g, ss, rs, dev)
        source = chip_dn if way == 0 else chip_up
        if kind == 3:
            source = source + flip
        return block_copy(source, g, ss, rs, dev, lo if way == 0 else hi)

    def send_own(g):
        z_copy(0, g, 0).start()
        z_copy(0, g, 1).start()
        own_y(g).start()

    def send_partner(g):
        own_y(g).wait_recv()
        z_copy(1, g, 0).start()
        z_copy(1, g, 1).start()

    def relay(kind, g):
        for way in (0, 1):
            z_copy(kind, g, way).wait_recv()
            z_copy(kind + 2, g, way).start()

    def finish(g):
        for way in (0, 1):
            z_copy(2, g, way).wait_recv()
            z_copy(3, g, way).wait_recv()

    def project(g):
        depth = 8 * HD
        at = pl.ds(g * depth, depth)
        rows_g = gath[:, g].reshape(256, depth)
        part = jnp.dot(rows_g, wown[at, :], preferred_element_type=F32)
        other = jnp.dot(rows_g, wsib[at, :], preferred_element_type=F32)
        if g == 0:
            acc[0] = part
            acc[1] = other
        else:
            acc[0] += part
            acc[1] += other

    attend(0)
    pl.semaphore_wait(barrier, 127)
    send_own(0)
    send_w = remote(w_hbm, wsib, sib_s.at[0], sib_r.at[0], sib)
    send_w.start()
    send_res = remote(res_ref.at[:, 1 - core], ressib, sib_s.at[1], sib_r.at[1], sib)
    send_res.start()
    gall_ref[e] = gain_ref[...]
    gains = [
        remote(gain_ref, gall_ref.at[e], gain_s.at[d], gain_r.at[d], (e + d) % 16)
        for d in range(1, 16)
    ]
    for gain in gains:
        gain.start()
    attend(1)
    send_own(1)
    send_partner(0)
    relay(0, 0)
    attend(2)
    send_own(2)
    relay(1, 0)
    send_partner(1)
    relay(0, 1)
    attend(3)
    send_own(3)
    relay(1, 1)
    send_partner(2)
    relay(0, 2)
    experts, seqs = slot_ref.shape
    which = lax.broadcasted_iota(jnp.int32, (experts, seqs), 0)
    named = jnp.zeros((experts, seqs), F32)
    weight = jnp.zeros((experts, seqs), F32)
    for k in range(8):
        same = which == ids_ref[k : k + 1, :]
        named = named + jnp.where(same, 1.0, 0.0)
        weight = weight + jnp.where(same, rw_ref[k : k + 1, :], 0.0)
    wt_ref[...] = weight
    early = lax.broadcasted_iota(jnp.int32, (seqs, seqs), 0)
    late = lax.broadcasted_iota(jnp.int32, (seqs, seqs), 1)
    ahead = jnp.where(early < late, 1.0, 0.0).astype(BF16)
    slots = jnp.dot(named.astype(BF16), ahead, preferred_element_type=F32)
    slot_ref[...] = jnp.where(named > 0.0, slots, -1.0)
    fetch_w.wait()
    send_w.wait_recv()
    finish(0)
    project(0)
    relay(1, 2)
    send_partner(3)
    relay(0, 3)
    finish(1)
    project(1)
    relay(1, 3)
    finish(2)
    project(2)
    finish(3)
    project(3)
    send_res.wait_recv()
    stage[...] = (ressib[...].astype(F32) + acc[1].reshape(8, 32, HD)).astype(BF16)
    send_out = remote(stage, att_ref.at[:, core], sib_s.at[2], sib_r.at[2], sib)
    send_out.start()
    att_ref[:, core] = (res_ref[:, core].astype(F32) + acc[0].reshape(8, 32, HD)).astype(BF16)
    send_out.wait_recv()

    place = lax.broadcasted_iota(jnp.int32, (SLOTS, seqs), 0).astype(F32)
    px, py = p // 2, p % 2

    def target(d):
        d = lax.rem(d * 37, 128)
        c = lax.rem(core + d, 2)
        d = lax.div(d, 2)
        zz = lax.rem(z + d, 4)
        d = lax.div(d, 4)
        yh = lax.rem(y_hi + d, 2)
        d = lax.div(d, 2)
        yl = lax.rem(py + d, 2)
        d = lax.div(d, 2)
        xx = lax.rem(px + d, 4)
        return xx * 2 + yl, yh * 8 + zz * 2 + c

    def out_copy(d):
        tp, te = target(d)
        return pltpu.make_async_remote_copy(
            src_ref=obuf.at[tp * 16 + te],
            dst_ref=rbuf.at[me],
            send_sem=out_s,
            recv_sem=out_r,
            device_id={"pool": tp, "expert": te},
            device_id_type=MESH,
        )

    def pick(i):
        places, parts = [], []
        for u in range(4):
            tp, te = target(i * 4 + u)
            t = tp * 16 + te
            places.append(t)
            parts.append(jnp.where(slot_ref[pl.ds(t, 1), :] == place, 1.0, 0.0).astype(BF16))
        chosen = jnp.concatenate(parts, axis=0)
        picked = jnp.dot(chosen, att_ref[...].reshape(seqs, HD), preferred_element_type=F32)
        return places, picked.astype(BF16)

    places, picked = pick(0)
    rbuf[me] = picked[0:SLOTS]
    for u in range(1, 4):
        obuf[places[u]] = picked[u * SLOTS : (u + 1) * SLOTS]

    def some(i, carry):
        places, picked = pick(i)
        for u in range(4):
            obuf[places[u]] = picked[u * SLOTS : (u + 1) * SLOTS]
        for u in range(4):
            out_copy(i * 4 + u - 3).start()
        return carry

    lax.fori_loop(1, 32, some, 0)
    for u in range(3):
        out_copy(125 + u).start()

    everyone = pl.ds(0, 127)
    out_all = pltpu.make_async_remote_copy(
        src_ref=obuf.at[everyone],
        dst_ref=rbuf.at[everyone],
        send_sem=out_s,
        recv_sem=out_r,
        device_id={"pool": p, "expert": sib},
        device_id_type=MESH,
    )
    for gain in gains:
        gain.wait()
    gain_row = jnp.concatenate([gall_ref[f] for f in range(16)], axis=1)
    out_all.wait_recv()

    def norm(i, carry):
        at = pl.ds(pl.multiple_of(lax.rem(i, 4) * 16, 16), 16)
        first = lax.div(i, 4) * 16
        x = jnp.concatenate([rbuf[first + f, at, :] for f in range(16)], axis=1).astype(F32)
        inv = lax.rsqrt(jnp.sum(x * x, axis=1, keepdims=True) / (16 * HD) + EPS)
        xs[pl.ds(pl.multiple_of(i * 16, 16), 16), :] = (x * inv * gain_row).astype(BF16)
        return carry

    lax.fori_loop(0, 32, norm, 0)
    ffn[0].wait()
    ffn[1].wait()

    def up(i, carry):
        at = pl.ds(pl.multiple_of(i * 256, 256), 256)
        gate = jnp.dot(xs[...], gw[:, at], preferred_element_type=F32)
        upper = jnp.dot(xs[...], uw[:, at], preferred_element_type=F32)
        hid[:, at] = (gate / (1.0 + jnp.exp(-gate)) * upper).astype(BF16)
        return carry

    lax.fori_loop(0, 3, up, 0)
    ffn[2].wait()

    def back_copy(i, pp, h):
        tp = lax.rem(p + pp, 8)
        te = lax.rem(chip + i, 8) * 2 + lax.rem(core + h, 2)
        return pltpu.make_async_remote_copy(
            src_ref=ybuf.at[tp * 16 + te],
            dst_ref=zbuf.at[me],
            send_sem=back_s,
            recv_sem=back_r.at[i],
            device_id={"pool": tp, "expert": te},
            device_id_type=MESH,
        )

    def send_back(i, own):
        for pp in range(8):
            for h in range(2):
                if not (own and pp == 0 and h == 0):
                    back_copy(i, pp, h).start()

    def down(i):
        tile = lax.rem(chip + i, 8)
        at = pl.ds(pl.multiple_of(tile * 256, 256), 256)
        y = jnp.dot(hid[...], dw[:, at], preferred_element_type=F32).astype(BF16)
        for pp in range(8):
            for h in range(2):
                ybuf[pp * 16 + tile * 2 + h] = y[
                    pp * SLOTS : (pp + 1) * SLOTS, h * HD : (h + 1) * HD
                ]

    down(0)
    down(1)
    send_back(0, True)

    def downs(i, carry):
        down(i)
        send_back(i - 1, False)
        return carry

    lax.fori_loop(2, 8, downs, 0)
    send_back(7, False)
    zbuf[me] = ybuf[me]

    mixt[...] = jnp.zeros_like(mixt)

    def gather_back(i, carry):
        first = lax.rem(chip + 8 - i, 8) * 2
        for c in range(4):
            parts, ys = [], []
            for pp in (2 * c, 2 * c + 1):
                for h in range(2):
                    t = pp * 16 + first + h
                    parts.append(
                        jnp.where(
                            slot_ref[pl.ds(t, 1), :] == place, wt_ref[pl.ds(t, 1), :], 0.0
                        ).astype(BF16)
                    )
                    ys.append(zbuf[t])
            chosen = jnp.concatenate(parts, axis=0)
            y = jnp.concatenate(ys, axis=0)
            mixt[...] += lax.dot_general(y, chosen, TN, preferred_element_type=F32)
        return carry

    def back_all(i, number):
        return pltpu.make_async_remote_copy(
            src_ref=ybuf.at[pl.ds(0, number)],
            dst_ref=zbuf.at[pl.ds(0, number)],
            send_sem=back_s,
            recv_sem=back_r.at[i],
            device_id={"pool": p, "expert": sib},
            device_id_type=MESH,
        )

    back_all(0, 15).wait_recv()
    gather_back(0, 0)

    def collect(i, carry):
        back_all(i, 16).wait_recv()
        return gather_back(i, carry)

    lax.fori_loop(1, 8, collect, 0)
    mix_ref[...] = mixt[...].T.astype(BF16)
    out_all.wait_send()
    back_all(0, 127).wait_send()
    for g in range(4):
        own_y(g).wait_send()
        for kind in range(4):
            z_copy(kind, g, 0).wait_send()
            z_copy(kind, g, 1).wait_send()
    send_w.wait_send()
    send_res.wait_send()
    send_out.wait_send()


def shards(
    queries,
    kv_cache,
    block_index,
    lengths,
    residual,
    out_weight,
    norm_gain,
    expert_ids,
    route_weights,
    gate_weight,
    up_weight,
    down_weight,
):
    rows = queries.shape[0]
    span = kv_cache.shape[0] * kv_cache.shape[1]
    width = kv_cache.shape[2]
    wide, hidden = gate_weight.shape[1:]
    dma = pltpu.SemaphoreType.DMA
    att, mixed = pl.pallas_call(
        layer,
        out_shape=(
            jax.ShapeDtypeStruct((8, 2, 32, HD), BF16),
            jax.ShapeDtypeStruct((512, HD), BF16),
        ),
        in_specs=[VM, ANY, VM, VM, VM, ANY, VM, VM, VM, ANY, ANY, ANY],
        out_specs=(VM, VM),
        scratch_shapes=[
            pltpu.VMEM((width // HD, span, HD), BF16),
            pltpu.VMEM(out_weight.shape, BF16),
            pltpu.VMEM(out_weight.shape, BF16),
            pltpu.VMEM((8, 32, HD), BF16),
            pltpu.VMEM((8, 4, 32, 8 * HD), BF16),
            pltpu.VMEM((256, span), F32),
            pltpu.VMEM((256, span), BF16),
            pltpu.VMEM((256, HD), F32),
            pltpu.VMEM((rows, span), F32),
            pltpu.VMEM((8, 32, HD), BF16),
            pltpu.VMEM((2, 256, HD), F32),
            pltpu.VMEM((128, 128), jnp.int32),
            pltpu.VMEM((16, 1, HD), F32),
            pltpu.VMEM((128, 512), F32),
            pltpu.VMEM((128, 512), F32),
            pltpu.VMEM((wide, hidden), BF16),
            pltpu.VMEM((wide, hidden), BF16),
            pltpu.VMEM((hidden, wide), BF16),
            pltpu.VMEM((128, SLOTS, HD), BF16),
            pltpu.VMEM((128, SLOTS, HD), BF16),
            pltpu.VMEM((128, SLOTS, HD), BF16),
            pltpu.VMEM((128, SLOTS, HD), BF16),
            pltpu.VMEM((512, wide), BF16),
            pltpu.VMEM((512, hidden), BF16),
            pltpu.VMEM((HD, 512), F32),
            dma((8,)),
            dma,
            dma((4,)),
            dma((4,)),
            dma((4, 4, 2)),
            dma((4, 4, 2)),
            dma((3,)),
            dma((3,)),
            dma((16,)),
            dma((16,)),
            dma((3,)),
            dma,
            dma,
            dma,
            dma((8,)),
        ],
        compiler_params=pltpu.CompilerParams(
            collective_id=0, has_side_effects=True, vmem_limit_bytes=60 * 1024 * 1024
        ),
        name="layer",
    )(
        queries,
        kv_cache.reshape(span, width),
        block_index.T,
        lengths.reshape(1, rows),
        residual.reshape(8, 2, 32, HD),
        out_weight,
        norm_gain.reshape(1, HD),
        expert_ids.T,
        route_weights.T,
        gate_weight,
        up_weight,
        down_weight,
    )
    return (att.reshape(512, HD), mixed)


def solution(mesh):
    return jax.shard_map(
        shards,
        mesh=mesh,
        in_specs=(
            P(("pool", "expert"), None),
            P(("pool", "expert"), None, None),
            P(("pool", "expert"), None),
            P(("pool", "expert")),
            P("pool", "expert"),
            P(None, "expert"),
            P("expert"),
            P("pool", None),
            P("pool", None),
            P(("pool", "expert"), None, None),
            P(("pool", "expert"), None, None),
            P(("pool", "expert"), None, None),
        ),
        out_specs=(P("pool", "expert"), P("pool", "expert")),
        check_vma=False,
    )
```

time: 150 us -> 117 us (0.78)
  blocking collectives: 73.5 us -> 0 us
  Pallas kernels: 72.3 us -> 113 us
    all_to_all x2 -> x0, blocking collectives: 73.5 us -> none  [the longest x1 37.8 us: shards(): lax.all_to_all(outgoing.reshape(128, 64, HD), axes, 0, 0, tiled=True)]
    pallas_call x4 -> x1, Pallas kernels: 72.3 us -> 113 us  [shards(): pl.pallas_call(layer, out_shape=(jax.ShapeDtypeStruct((8, 2, 32, HD), BF1...]
    unnamed x4 -> x2, local copies, waits for them, and re-layouts: 2.03 us -> 3.14 us
where the time goes in v2:
time: 117 us; the launch traced here: 116 us
  Pallas kernels  113 us (97%)
  local copies, waits for them, and re-layouts  3.14 us (3%)
    pallas_call x1, Pallas kernels, shards(): pl.pallas_call(layer, out_shape=(jax.ShapeDtypeStruct((8, 2, 32, HD), BF1...  113 us
    unnamed x2, local copies, waits for them, and re-layouts  3.14 us

profile of v2, /device:TPU:1, one launch (start us, length us, event | category | flops | bytes accessed | tf_op | source)
XLA Modules:
  0.0 116.5 jit_solution(14072139394680741532)
XLA Ops:
  0.6 112.7 %layer.1 = (bf16[8,2,32,128]{3,2,1,0:T(8,128)(2,1)}, bf16[512,128]{1,0:T(8,128)(2,1)}) custom-call(bf16[32,4096]{1,0:T(8,128)(2,1)} %q_ref.1, bf16[2048,1024]{1,0:T(8,128)(2,1)} %bitcast.8, s32[8,32]{1,0:T(8,128)} %bitcast.13, s32[1,32]{1,0:T(1,128)} %bitcast.14, bf16[8,2,32,128]{3,2,1,0:T(8,128)(2,1)} %bitcast.9, bf16[4096,128]{1,0:T(8,128)(2,1)} %w_hbm.1, ...), custom_call_target="tpu_custom_call" | custom-call | tf_op jit(solution)/shard_map/layer/pallas_call | solution.py:498
  113.3 1.6 %copy.16 = bf16[512,128]{1,0:T(8,128)(2,1)} copy(bf16[512,128]{1,0:T(8,128)(2,1)} %bitcast.10) | data formatting | bytes 262144
  114.9 1.6 %copy.17 = bf16[512,128]{1,0:T(8,128)(2,1)} copy(bf16[512,128]{1,0:T(8,128)(2,1)} %get-tuple-element.9) | data formatting | bytes 262144

commit v3 on v2

--- a/solution.py
+++ b/solution.py
@@ -104,14 +104,11 @@
     for g in range(4):
         fetch(g).start()
         fetch(4 + g).start()
-    fetch_w.start()
     ffn = [
         pltpu.make_async_copy(g_hbm.at[0], gw, ffn_sem.at[0]),
         pltpu.make_async_copy(u_hbm.at[0], uw, ffn_sem.at[1]),
         pltpu.make_async_copy(d_hbm.at[0], dw, ffn_sem.at[2]),
     ]
-    for copy in ffn:
-        copy.start()
 
     def greet(d, carry):
         t = lax.rem(me + d, 128)
@@ -149,17 +146,17 @@
         s_scr[...] = lax.dot_general(query, kv[g], NT, preferred_element_type=F32)
 
         def soften(r, carry):
-            at = pl.ds(pl.multiple_of(r * 16, 16), 16)
-            of = pl.ds(pl.multiple_of((r % 2) * 16, 16), 16)
-            x = s_scr[at, :] * factor + bias[of, :]
-            top = jnp.max(x, axis=1, keepdims=True)
-            ex = jnp.exp2(x - top)
-            total = jnp.sum(ex, axis=1, keepdims=True)
-            p_scr[at, :] = ex.astype(BF16)
-            linv[at, :] = jnp.broadcast_to(1.0 / total, (16, HD))
-            return carry
-
-        lax.fori_loop(0, 16, soften, 0)
+            for v in range(4):
+                at = pl.ds(pl.multiple_of(r * 64 + v * 16, 16), 16)
+                x = s_scr[at, :] * factor + bias[(v % 2) * 16 : (v % 2) * 16 + 16, :]
+                top = jnp.max(x, axis=1, keepdims=True)
+                ex = jnp.exp2(x - top)
+                total = jnp.sum(ex, axis=1, keepdims=True)
+                p_scr[at, :] = ex.astype(BF16)
+                linv[at, :] = jnp.broadcast_to(1.0 / total, (16, HD))
+            return carry
+
+        lax.fori_loop(0, 4, soften, 0)
         fetch(4 + g).wait()
         o = jnp.dot(p_scr[...], kv[4 + g], preferred_element_type=F32) * linv[...]
         o = o.astype(BF16)
@@ -231,6 +228,7 @@
             acc[1] += other
 
     attend(0)
+    fetch_w.start()
     pl.semaphore_wait(barrier, 127)
     send_own(0)
     send_w = remote(w_hbm, wsib, sib_s.at[0], sib_r.at[0], sib)
@@ -245,6 +243,8 @@
     for gain in gains:
         gain.start()
     attend(1)
+    for copy in ffn:
+        copy.start()
     send_own(1)
     send_partner(0)
     relay(0, 0)
@@ -296,176 +296,183 @@
     place = lax.broadcasted_iota(jnp.int32, (SLOTS, seqs), 0).astype(F32)
     px, py = p // 2, p % 2
 
-    def target(d):
-        d = lax.rem(d * 37, 128)
-        c = lax.rem(core + d, 2)
+    def place_of(xx, yl, yh, zz, c):
+        return (xx * 2 + yl) * 16 + yh * 8 + zz * 2 + c
+
+    def digits(d):
+        d = lax.rem(d * 37, 64)
+        c = lax.rem(d, 2)
         d = lax.div(d, 2)
-        zz = lax.rem(z + d, 4)
+        dz = lax.rem(d, 4)
         d = lax.div(d, 4)
-        yh = lax.rem(y_hi + d, 2)
+        dh = lax.rem(d, 2)
         d = lax.div(d, 2)
-        yl = lax.rem(py + d, 2)
-        d = lax.div(d, 2)
-        xx = lax.rem(px + d, 4)
-        return xx * 2 + yl, yh * 8 + zz * 2 + c
-
-    def out_copy(d):
-        tp, te = target(d)
+        return c, dz, dh, lax.rem(d, 2), lax.div(d, 2)
+
+    def target(half, d):
+        c, dz, dh, dl, dx = digits(d)
+        return place_of(
+            lax.rem(px + 2 * dx + half, 4),
+            lax.rem(py + dl, 2),
+            lax.rem(y_hi + dh, 2),
+            lax.rem(z + dz, 4),
+            lax.rem(core + c, 2),
+        )
+
+    def origin(half, d):
+        c, dz, dh, dl, dx = digits(d)
+        return place_of(
+            lax.rem(px + 8 - 2 * dx - half, 4),
+            lax.rem(py + dl, 2),
+            lax.rem(y_hi + dh, 2),
+            lax.rem(z + 4 - dz, 4),
+            lax.rem(core + c, 2),
+        )
+
+    def send_to(t, src, dst, ssem, rsem):
         return pltpu.make_async_remote_copy(
-            src_ref=obuf.at[tp * 16 + te],
-            dst_ref=rbuf.at[me],
-            send_sem=out_s,
-            recv_sem=out_r,
-            device_id={"pool": tp, "expert": te},
+            src_ref=src,
+            dst_ref=dst,
+            send_sem=ssem,
+            recv_sem=rsem,
+            device_id={"pool": lax.div(t, 16), "expert": lax.rem(t, 16)},
             device_id_type=MESH,
         )
 
-    def pick(i):
+    def out_copy(half, d):
+        t = target(half, d)
+        return send_to(t, obuf.at[t], rbuf.at[me], out_s, out_r.at[half])
+
+    def pick(half, i):
         places, parts = [], []
         for u in range(4):
-            tp, te = target(i * 4 + u)
-            t = tp * 16 + te
+            t = target(half, i * 4 + u)
             places.append(t)
             parts.append(jnp.where(slot_ref[pl.ds(t, 1), :] == place, 1.0, 0.0).astype(BF16))
         chosen = jnp.concatenate(parts, axis=0)
         picked = jnp.dot(chosen, att_ref[...].reshape(seqs, HD), preferred_element_type=F32)
         return places, picked.astype(BF16)
 
-    places, picked = pick(0)
+    places, picked = pick(0, 0)
     rbuf[me] = picked[0:SLOTS]
     for u in range(1, 4):
         obuf[places[u]] = picked[u * SLOTS : (u + 1) * SLOTS]
 
-    def some(i, carry):
-        places, picked = pick(i)
-        for u in range(4):
-            obuf[places[u]] = picked[u * SLOTS : (u + 1) * SLOTS]
-        for u in range(4):
-            out_copy(i * 4 + u - 3).start()
-        return carry
-
-    lax.fori_loop(1, 32, some, 0)
-    for u in range(3):
-        out_copy(125 + u).start()
-
-    everyone = pl.ds(0, 127)
-    out_all = pltpu.make_async_remote_copy(
-        src_ref=obuf.at[everyone],
-        dst_ref=rbuf.at[everyone],
-        send_sem=out_s,
-        recv_sem=out_r,
-        device_id={"pool": p, "expert": sib},
-        device_id_type=MESH,
-    )
+    def some(half):
+        def step(i, carry):
+            places, picked = pick(half, i)
+            for u in range(4):
+                obuf[places[u]] = picked[u * SLOTS : (u + 1) * SLOTS]
+            for u in range(4):
+                out_copy(half, i * 4 + u - 3).start()
+            return carry
+
+        return step
+
+    lax.fori_loop(1, 16, some(0), 0)
+    for u in range(61, 64):
+        out_copy(0, u).start()
+    places, picked = pick(1, 0)
+    for u in range(4):
+        obuf[places[u]] = picked[u * SLOTS : (u + 1) * SLOTS]
+    out_copy(1, 0).start()
+    lax.fori_loop(1, 16, some(1), 0)
+    for u in range(61, 64):
+        out_copy(1, u).start()
+
+    def many(src, dst, ssem, rsem, number):
+        return send_to(
+            p * 16 + sib, src.at[pl.ds(0, number)], dst.at[pl.ds(0, number)], ssem, rsem
+        )
+
     for gain in gains:
         gain.wait()
     gain_row = jnp.concatenate([gall_ref[f] for f in range(16)], axis=1)
-    out_all.wait_recv()
-
-    def norm(i, carry):
-        at = pl.ds(pl.multiple_of(lax.rem(i, 4) * 16, 16), 16)
-        first = lax.div(i, 4) * 16
-        x = jnp.concatenate([rbuf[first + f, at, :] for f in range(16)], axis=1).astype(F32)
-        inv = lax.rsqrt(jnp.sum(x * x, axis=1, keepdims=True) / (16 * HD) + EPS)
-        xs[pl.ds(pl.multiple_of(i * 16, 16), 16), :] = (x * inv * gain_row).astype(BF16)
-        return carry
-
-    lax.fori_loop(0, 32, norm, 0)
-    ffn[0].wait()
-    ffn[1].wait()
-
-    def up(i, carry):
-        at = pl.ds(pl.multiple_of(i * 256, 256), 256)
-        gate = jnp.dot(xs[...], gw[:, at], preferred_element_type=F32)
-        upper = jnp.dot(xs[...], uw[:, at], preferred_element_type=F32)
-        hid[:, at] = (gate / (1.0 + jnp.exp(-gate)) * upper).astype(BF16)
-        return carry
-
-    lax.fori_loop(0, 3, up, 0)
-    ffn[2].wait()
-
-    def back_copy(i, pp, h):
-        tp = lax.rem(p + pp, 8)
-        te = lax.rem(chip + i, 8) * 2 + lax.rem(core + h, 2)
-        return pltpu.make_async_remote_copy(
-            src_ref=ybuf.at[tp * 16 + te],
-            dst_ref=zbuf.at[me],
-            send_sem=back_s,
-            recv_sem=back_r.at[i],
-            device_id={"pool": tp, "expert": te},
-            device_id_type=MESH,
-        )
-
-    def send_back(i, own):
-        for pp in range(8):
-            for h in range(2):
-                if not (own and pp == 0 and h == 0):
-                    back_copy(i, pp, h).start()
-
-    def down(i):
-        tile = lax.rem(chip + i, 8)
-        at = pl.ds(pl.multiple_of(tile * 256, 256), 256)
-        y = jnp.dot(hid[...], dw[:, at], preferred_element_type=F32).astype(BF16)
-        for pp in range(8):
-            for h in range(2):
-                ybuf[pp * 16 + tile * 2 + h] = y[
-                    pp * SLOTS : (pp + 1) * SLOTS, h * HD : (h + 1) * HD
-                ]
-
-    down(0)
-    down(1)
-    send_back(0, True)
-
-    def downs(i, carry):
-        down(i)
-        send_back(i - 1, False)
-        return carry
-
-    lax.fori_loop(2, 8, downs, 0)
-    send_back(7, False)
+
+    def back_copy(half, d):
+        t = target(half, d)
+        return send_to(t, ybuf.at[t], zbuf.at[me], back_s, back_r.at[half * 4 + lax.div(d, 16)])
+
+    def experts_of(half):
+        low = lax.rem(px + half, 2) * 2
+        many(obuf, rbuf, out_s, out_r.at[half], 63 + half).wait_recv()
+
+        def norm(i, carry):
+            q = lax.div(i, 4)
+            first = (low + lax.rem(q, 2) + lax.div(q, 2) * 4) * 16
+            at = pl.ds(pl.multiple_of(lax.rem(i, 4) * 16, 16), 16)
+            x = jnp.concatenate([rbuf[first + f, at, :] for f in range(16)], axis=1).astype(F32)
+            inv = lax.rsqrt(jnp.sum(x * x, axis=1, keepdims=True) / (16 * HD) + EPS)
+            xs[pl.ds(pl.multiple_of(i * 16, 16), 16), :] = (x * inv * gain_row).astype(BF16)
+            return carry
+
+        lax.fori_loop(0, 16, norm, 0)
+        if half == 0:
+            ffn[0].wait()
+            ffn[1].wait()
+
+        def up(i, carry):
+            at = pl.ds(pl.multiple_of(i * 256, 256), 256)
+            gate = jnp.dot(xs[...], gw[:, at], preferred_element_type=F32)
+            upper = jnp.dot(xs[...], uw[:, at], preferred_element_type=F32)
+            hid[:, at] = (gate / (1.0 + jnp.exp(-gate)) * upper).astype(BF16)
+            return carry
+
+        lax.fori_loop(0, 3, up, 0)
+        if half == 0:
+            ffn[2].wait()
+
+        def down(tile, carry):
+            at = pl.ds(pl.multiple_of(tile * 256, 256), 256)
+            y = jnp.dot(hid[...], dw[:, at], preferred_element_type=F32).astype(BF16)
+            for q in range(4):
+                first = (low + q % 2 + (q // 2) * 4) * 16
+                for h in range(2):
+                    ybuf[first + tile * 2 + h] = y[
+                        q * SLOTS : (q + 1) * SLOTS, h * HD : (h + 1) * HD
+                    ]
+            return carry
+
+        lax.fori_loop(0, 8, down, 0)
+
+        def send(d, carry):
+            back_copy(half, d).start()
+            return carry
+
+        lax.fori_loop(1 - half, 64, send, 0)
+
+    experts_of(0)
+    experts_of(1)
     zbuf[me] = ybuf[me]
 
     mixt[...] = jnp.zeros_like(mixt)
 
-    def gather_back(i, carry):
-        first = lax.rem(chip + 8 - i, 8) * 2
-        for c in range(4):
+    def gather_back(half, k):
+        many(ybuf, zbuf, back_s, back_r.at[half * 4 + k], 15 if half + k == 0 else 16).wait_recv()
+
+        def four(c, carry):
             parts, ys = [], []
-            for pp in (2 * c, 2 * c + 1):
-                for h in range(2):
-                    t = pp * 16 + first + h
-                    parts.append(
-                        jnp.where(
-                            slot_ref[pl.ds(t, 1), :] == place, wt_ref[pl.ds(t, 1), :], 0.0
-                        ).astype(BF16)
-                    )
-                    ys.append(zbuf[t])
+            for u in range(4):
+                t = origin(half, k * 16 + c * 4 + u)
+                parts.append(
+                    jnp.where(
+                        slot_ref[pl.ds(t, 1), :] == place, wt_ref[pl.ds(t, 1), :], 0.0
+                    ).astype(BF16)
+                )
+                ys.append(zbuf[t])
             chosen = jnp.concatenate(parts, axis=0)
             y = jnp.concatenate(ys, axis=0)
             mixt[...] += lax.dot_general(y, chosen, TN, preferred_element_type=F32)
-        return carry
-
-    def back_all(i, number):
-        return pltpu.make_async_remote_copy(
-            src_ref=ybuf.at[pl.ds(0, number)],
-            dst_ref=zbuf.at[pl.ds(0, number)],
-            send_sem=back_s,
-            recv_sem=back_r.at[i],
-            device_id={"pool": p, "expert": sib},
-            device_id_type=MESH,
-        )
-
-    back_all(0, 15).wait_recv()
-    gather_back(0, 0)
-
-    def collect(i, carry):
-        back_all(i, 16).wait_recv()
-        return gather_back(i, carry)
-
-    lax.fori_loop(1, 8, collect, 0)
+            return carry
+
+        lax.fori_loop(0, 4, four, 0)
+
+    for half in range(2):
+        for k in range(4):
+            gather_back(half, k)
     mix_ref[...] = mixt[...].T.astype(BF16)
-    out_all.wait_send()
-    back_all(0, 127).wait_send()
+    many(obuf, rbuf, out_s, out_r.at[0], 127).wait_send()
+    many(ybuf, zbuf, back_s, back_r.at[0], 127).wait_send()
     for g in range(4):
         own_y(g).wait_send()
         for kind in range(4):
@@ -526,8 +533,8 @@
             pltpu.VMEM((128, SLOTS, HD), BF16),
             pltpu.VMEM((128, SLOTS, HD), BF16),
             pltpu.VMEM((128, SLOTS, HD), BF16),
-            pltpu.VMEM((512, wide), BF16),
-            pltpu.VMEM((512, hidden), BF16),
+            pltpu.VMEM((256, wide), BF16),
+            pltpu.VMEM((256, hidden), BF16),
             pltpu.VMEM((HD, 512), F32),
             dma((8,)),
             dma,
@@ -541,7 +548,7 @@
             dma((16,)),
             dma((3,)),
             dma,
-            dma,
+            dma((2,)),
             dma,
             dma((8,)),
         ],

time: 117 us -> 97.8 us (0.84)
  Pallas kernels: 113 us -> 92.3 us
    pallas_call x1, Pallas kernels: 113 us -> 92.3 us  [shards(): pl.pallas_call(layer, out_shape=(jax.ShapeDtypeStruct((8, 2, 32, HD), BF1...]
where the time goes in v3:
time: 97.8 us; the launch traced here: 96.1 us
  Pallas kernels  92.3 us (94%)
  local copies, waits for them, and re-layouts  3.14 us (3%)
    pallas_call x1, Pallas kernels, shards(): pl.pallas_call(layer, out_shape=(jax.ShapeDtypeStruct((8, 2, 32, HD), BF1...  92.3 us
    unnamed x2, local copies, waits for them, and re-layouts  3.14 us

profile of v3, /device:TPU:1, one launch (start us, length us, event | category | flops | bytes accessed | tf_op | source)
XLA Modules:
  0.0 96.1 jit_solution(734156526245152318)
XLA Ops:
  0.6 92.3 %layer.1 = (bf16[8,2,32,128]{3,2,1,0:T(8,128)(2,1)}, bf16[512,128]{1,0:T(8,128)(2,1)}) custom-call(bf16[32,4096]{1,0:T(8,128)(2,1)} %q_ref.1, bf16[2048,1024]{1,0:T(8,128)(2,1)} %bitcast.8, s32[8,32]{1,0:T(8,128)} %bitcast.13, s32[1,32]{1,0:T(1,128)} %bitcast.14, bf16[8,2,32,128]{3,2,1,0:T(8,128)(2,1)} %bitcast.9, bf16[4096,128]{1,0:T(8,128)(2,1)} %w_hbm.1, ...), custom_call_target="tpu_custom_call" | custom-call | tf_op jit(solution)/shard_map/layer/pallas_call | solution.py:505
  93.0 1.6 %copy.16 = bf16[512,128]{1,0:T(8,128)(2,1)} copy(bf16[512,128]{1,0:T(8,128)(2,1)} %bitcast.10) | data formatting | bytes 262144
  94.5 1.6 %copy.17 = bf16[512,128]{1,0:T(8,128)(2,1)} copy(bf16[512,128]{1,0:T(8,128)(2,1)} %get-tuple-element.9) | data formatting | bytes 262144

commit v4 on v3

--- a/solution.py
+++ b/solution.py
@@ -74,6 +74,8 @@
     out_r,
     back_s,
     back_r,
+    ym_s,
+    ym_r,
 ):
     p = lax.axis_index("pool")
     e = lax.axis_index("expert")
@@ -214,6 +216,28 @@
             z_copy(2, g, way).wait_recv()
             z_copy(3, g, way).wait_recv()
 
+    def y_more(kind, g):
+        ss, rs = ym_s.at[kind, g], ym_r.at[kind, g]
+        if kind < 2:
+            return block_copy(chip_up if kind else chip_dn, g, ss, rs, dev_y)
+        return block_copy(chip_op, g, ss, rs, dev_y, hi if kind == 3 else lo)
+
+    def first_z(g):
+        for way in (0, 1):
+            z_copy(0, g, way).wait_recv()
+            z_copy(2, g, way).start()
+            y_more(way, g).start()
+
+    def second_z(g):
+        for way in (0, 1):
+            z_copy(2, g, way).wait_recv()
+            y_more(2 + way, g).start()
+
+    def finish_y(g):
+        own_y(g).wait_recv()
+        for kind in range(4):
+            y_more(kind, g).wait_recv()
+
     def project(g):
         depth = 8 * HD
         at = pl.ds(g * depth, depth)
@@ -246,18 +270,14 @@
     for copy in ffn:
         copy.start()
     send_own(1)
-    send_partner(0)
-    relay(0, 0)
     attend(2)
     send_own(2)
-    relay(1, 0)
-    send_partner(1)
-    relay(0, 1)
+    first_z(0)
     attend(3)
     send_own(3)
-    relay(1, 1)
+    first_z(1)
+    second_z(0)
     send_partner(2)
-    relay(0, 2)
     experts, seqs = slot_ref.shape
     which = lax.broadcasted_iota(jnp.int32, (experts, seqs), 0)
     named = jnp.zeros((experts, seqs), F32)
@@ -272,16 +292,18 @@
     ahead = jnp.where(early < late, 1.0, 0.0).astype(BF16)
     slots = jnp.dot(named.astype(BF16), ahead, preferred_element_type=F32)
     slot_ref[...] = jnp.where(named > 0.0, slots, -1.0)
+    relay(0, 2)
+    second_z(1)
+    send_partner(3)
     fetch_w.wait()
     send_w.wait_recv()
-    finish(0)
+    relay(0, 3)
+    relay(1, 2)
+    finish_y(0)
     project(0)
-    relay(1, 2)
-    send_partner(3)
-    relay(0, 3)
-    finish(1)
+    relay(1, 3)
+    finish_y(1)
     project(1)
-    relay(1, 3)
     finish(2)
     project(2)
     finish(3)
@@ -475,12 +497,20 @@
     many(ybuf, zbuf, back_s, back_r.at[0], 127).wait_send()
     for g in range(4):
         own_y(g).wait_send()
-        for kind in range(4):
+        for kind in (0, 2) if g < 2 else range(4):
             z_copy(kind, g, 0).wait_send()
             z_copy(kind, g, 1).wait_send()
+        if g < 2:
+            for kind in range(4):
+                y_more(kind, g).wait_send()
     send_w.wait_send()
     send_res.wait_send()
     send_out.wait_send()
+
+
+def hand_over(a_ref, b_ref, c_ref, d_ref):
+    c_ref[...] = a_ref[...]
+    d_ref[...] = b_ref[...]
 
 
 def shards(
@@ -551,6 +581,8 @@
             dma((2,)),
             dma,
             dma((8,)),
+            dma((4, 2)),
+            dma((4, 2)),
         ],
         compiler_params=pltpu.CompilerParams(
             collective_id=0, has_side_effects=True, vmem_limit_bytes=60 * 1024 * 1024
@@ -570,7 +602,16 @@
         up_weight,
         down_weight,
     )
-    return (att.reshape(512, HD), mixed)
+    return pl.pallas_call(
+        hand_over,
+        out_shape=(
+            jax.ShapeDtypeStruct((512, HD), BF16),
+            jax.ShapeDtypeStruct((512, HD), BF16),
+        ),
+        in_specs=[VM, VM],
+        out_specs=(VM, VM),
+        name="hand_over",
+    )(att.reshape(512, HD), mixed)
 
 
 def solution(mesh):

time: 97.8 us -> 92.7 us (0.948)
  local copies, waits for them, and re-layouts: 3.14 us -> 0 us
  Pallas kernels: 92.3 us -> 91.3 us
    unnamed x2 -> x0, local copies, waits for them, and re-layouts: 3.14 us -> none
    pallas_call x1, Pallas kernels: 92.3 us -> 89.6 us  [shards(): pl.pallas_call(layer, out_shape=(jax.ShapeDtypeStruct((8, 2, 32, HD), BF1...]
    pallas_call x0 -> x1, Pallas kernels: none -> 1.68 us  [shards(): pl.pallas_call(hand_over, out_shape=(jax.ShapeDtypeStruct((512, HD), BF16...]
where the time goes in v4:
time: 92.7 us; the launch traced here: 91.9 us
  Pallas kernels  91.3 us (98%)
    pallas_call x1, Pallas kernels, shards(): pl.pallas_call(layer, out_shape=(jax.ShapeDtypeStruct((8, 2, 32, HD), BF1...  89.6 us

profile of v4, /device:TPU:1, one launch (start us, length us, event | category | flops | bytes accessed | tf_op | source)
XLA Modules:
  0.0 91.9 jit_solution(4003602321258950630)
XLA Ops:
  0.6 89.6 %layer.1 = (bf16[8,2,32,128]{3,2,1,0:T(8,128)(2,1)}, bf16[512,128]{1,0:T(8,128)(2,1)}) custom-call(bf16[32,4096]{1,0:T(8,128)(2,1)} %q_ref.1, bf16[2048,1024]{1,0:T(8,128)(2,1)} %bitcast.8, s32[8,32]{1,0:T(8,128)} %bitcast.13, s32[1,32]{1,0:T(1,128)} %bitcast.14, bf16[8,2,32,128]{3,2,1,0:T(8,128)(2,1)} %bitcast.9, bf16[4096,128]{1,0:T(8,128)(2,1)} %w_hbm.1, ...), custom_call_target="tpu_custom_call" | custom-call | tf_op jit(solution)/shard_map/layer/pallas_call | solution.py:535
  90.2 1.7 %hand_over.1 = (bf16[512,128]{1,0:T(8,128)(2,1)}, bf16[512,128]{1,0:T(8,128)(2,1)}) custom-call(bf16[512,128]{1,0:T(8,128)(2,1)} %bitcast.10, bf16[512,128]{1,0:T(8,128)(2,1)} %get-tuple-element.5.b_ref), custom_call_target="tpu_custom_call" | custom-call | tf_op jit(solution)/shard_map/hand_over/pallas_call | solution.py:605

commit v5 on v4

--- a/solution.py
+++ b/solution.py
@@ -322,33 +322,28 @@
         return (xx * 2 + yl) * 16 + yh * 8 + zz * 2 + c
 
     def digits(d):
-        d = lax.rem(d * 37, 64)
+        d = lax.rem(d * 13, 32)
         c = lax.rem(d, 2)
         d = lax.div(d, 2)
         dz = lax.rem(d, 4)
         d = lax.div(d, 4)
-        dh = lax.rem(d, 2)
-        d = lax.div(d, 2)
-        return c, dz, dh, lax.rem(d, 2), lax.div(d, 2)
-
-    def target(half, d):
-        c, dz, dh, dl, dx = digits(d)
+        return c, dz, lax.rem(d, 2), lax.div(d, 2)
+
+    def there(q, w, way):
+        return lax.rem(px + 8 + way * q + 2 * w, 4), lax.rem(py + w, 2)
+
+    def target(q, d, way=1):
+        c, dz, dh, w = digits(d)
+        xx, yl = there(q, w, way)
         return place_of(
-            lax.rem(px + 2 * dx + half, 4),
-            lax.rem(py + dl, 2),
-            lax.rem(y_hi + dh, 2),
-            lax.rem(z + dz, 4),
-            lax.rem(core + c, 2),
+            xx, yl, lax.rem(y_hi + dh, 2), lax.rem(z + dz, 4), lax.rem(core + c, 2)
         )
 
-    def origin(half, d):
-        c, dz, dh, dl, dx = digits(d)
+    def origin(q, d):
+        c, dz, dh, w = digits(d)
+        xx, yl = there(q, w, 1)
         return place_of(
-            lax.rem(px + 8 - 2 * dx - half, 4),
-            lax.rem(py + dl, 2),
-            lax.rem(y_hi + dh, 2),
-            lax.rem(z + 4 - dz, 4),
-            lax.rem(core + c, 2),
+            xx, yl, lax.rem(y_hi + dh, 2), lax.rem(z + 4 - dz, 4), lax.rem(core + c, 2)
         )
 
     def send_to(t, src, dst, ssem, rsem):
@@ -361,14 +356,14 @@
             device_id_type=MESH,
         )
 
-    def out_copy(half, d):
-        t = target(half, d)
-        return send_to(t, obuf.at[t], rbuf.at[me], out_s, out_r.at[half])
-
-    def pick(half, i):
+    def out_copy(quarter, d):
+        t = target(quarter, d)
+        return send_to(t, obuf.at[t], rbuf.at[me], out_s, out_r.at[quarter])
+
+    def pick(quarter, i):
         places, parts = [], []
         for u in range(4):
-            t = target(half, i * 4 + u)
+            t = target(quarter, i * 4 + u)
             places.append(t)
             parts.append(jnp.where(slot_ref[pl.ds(t, 1), :] == place, 1.0, 0.0).astype(BF16))
         chosen = jnp.concatenate(parts, axis=0)
@@ -380,27 +375,28 @@
     for u in range(1, 4):
         obuf[places[u]] = picked[u * SLOTS : (u + 1) * SLOTS]
 
-    def some(half):
+    def some(quarter):
         def step(i, carry):
-            places, picked = pick(half, i)
+            places, picked = pick(quarter, i)
             for u in range(4):
                 obuf[places[u]] = picked[u * SLOTS : (u + 1) * SLOTS]
             for u in range(4):
-                out_copy(half, i * 4 + u - 3).start()
+                out_copy(quarter, i * 4 + u - 3).start()
             return carry
 
         return step
 
-    lax.fori_loop(1, 16, some(0), 0)
-    for u in range(61, 64):
+    lax.fori_loop(1, 8, some(0), 0)
+    for u in range(29, 32):
         out_copy(0, u).start()
-    places, picked = pick(1, 0)
-    for u in range(4):
-        obuf[places[u]] = picked[u * SLOTS : (u + 1) * SLOTS]
-    out_copy(1, 0).start()
-    lax.fori_loop(1, 16, some(1), 0)
-    for u in range(61, 64):
-        out_copy(1, u).start()
+    for q in range(1, 4):
+        places, picked = pick(q, 0)
+        for u in range(4):
+            obuf[places[u]] = picked[u * SLOTS : (u + 1) * SLOTS]
+        out_copy(q, 0).start()
+        lax.fori_loop(1, 8, some(q), 0)
+        for u in range(29, 32):
+            out_copy(q, u).start()
 
     def many(src, dst, ssem, rsem, number):
         return send_to(
@@ -411,25 +407,27 @@
         gain.wait()
     gain_row = jnp.concatenate([gall_ref[f] for f in range(16)], axis=1)
 
-    def back_copy(half, d):
-        t = target(half, d)
-        return send_to(t, ybuf.at[t], zbuf.at[me], back_s, back_r.at[half * 4 + lax.div(d, 16)])
-
-    def experts_of(half):
-        low = lax.rem(px + half, 2) * 2
-        many(obuf, rbuf, out_s, out_r.at[half], 63 + half).wait_recv()
+    def back_copy(quarter, d):
+        t = target(quarter, d, -1)
+        return send_to(t, ybuf.at[t], zbuf.at[me], back_s, back_r.at[quarter * 2 + lax.div(d, 16)])
+
+    def experts_of(quarter):
+        many(obuf, rbuf, out_s, out_r.at[quarter], 32 if quarter else 31).wait_recv()
+
+        def pool_of(w):
+            xx, yl = there(quarter, w, -1)
+            return (xx * 2 + yl) * 16
 
         def norm(i, carry):
-            q = lax.div(i, 4)
-            first = (low + lax.rem(q, 2) + lax.div(q, 2) * 4) * 16
+            first = pool_of(lax.div(i, 4))
             at = pl.ds(pl.multiple_of(lax.rem(i, 4) * 16, 16), 16)
             x = jnp.concatenate([rbuf[first + f, at, :] for f in range(16)], axis=1).astype(F32)
             inv = lax.rsqrt(jnp.sum(x * x, axis=1, keepdims=True) / (16 * HD) + EPS)
             xs[pl.ds(pl.multiple_of(i * 16, 16), 16), :] = (x * inv * gain_row).astype(BF16)
             return carry
 
-        lax.fori_loop(0, 16, norm, 0)
-        if half == 0:
+        lax.fori_loop(0, 8, norm, 0)
+        if quarter == 0:
             ffn[0].wait()
             ffn[1].wait()
 
@@ -441,14 +439,14 @@
             return carry
 
         lax.fori_loop(0, 3, up, 0)
-        if half == 0:
+        if quarter == 0:
             ffn[2].wait()
 
         def down(tile, carry):
             at = pl.ds(pl.multiple_of(tile * 256, 256), 256)
             y = jnp.dot(hid[...], dw[:, at], preferred_element_type=F32).astype(BF16)
-            for q in range(4):
-                first = (low + q % 2 + (q // 2) * 4) * 16
+            for q in range(2):
+                first = pool_of(q)
                 for h in range(2):
                     ybuf[first + tile * 2 + h] = y[
                         q * SLOTS : (q + 1) * SLOTS, h * HD : (h + 1) * HD
@@ -458,24 +456,24 @@
         lax.fori_loop(0, 8, down, 0)
 
         def send(d, carry):
-            back_copy(half, d).start()
+            back_copy(quarter, d).start()
             return carry
 
-        lax.fori_loop(1 - half, 64, send, 0)
-
-    experts_of(0)
-    experts_of(1)
+        lax.fori_loop(0 if quarter else 1, 32, send, 0)
+
+    for q in range(4):
+        experts_of(q)
     zbuf[me] = ybuf[me]
 
     mixt[...] = jnp.zeros_like(mixt)
 
-    def gather_back(half, k):
-        many(ybuf, zbuf, back_s, back_r.at[half * 4 + k], 15 if half + k == 0 else 16).wait_recv()
+    def gather_back(quarter, k):
+        many(ybuf, zbuf, back_s, back_r.at[quarter * 2 + k], 15 if quarter + k == 0 else 16).wait_recv()
 
         def four(c, carry):
             parts, ys = [], []
             for u in range(4):
-                t = origin(half, k * 16 + c * 4 + u)
+                t = origin(quarter, k * 16 + c * 4 + u)
                 parts.append(
                     jnp.where(
                         slot_ref[pl.ds(t, 1), :] == place, wt_ref[pl.ds(t, 1), :], 0.0
@@ -489,9 +487,9 @@
 
         lax.fori_loop(0, 4, four, 0)
 
-    for half in range(2):
-        for k in range(4):
-            gather_back(half, k)
+    for quarter in range(4):
+        for k in range(2):
+            gather_back(quarter, k)
     mix_ref[...] = mixt[...].T.astype(BF16)
     many(obuf, rbuf, out_s, out_r.at[0], 127).wait_send()
     many(ybuf, zbuf, back_s, back_r.at[0], 127).wait_send()
@@ -563,8 +561,8 @@
             pltpu.VMEM((128, SLOTS, HD), BF16),
             pltpu.VMEM((128, SLOTS, HD), BF16),
             pltpu.VMEM((128, SLOTS, HD), BF16),
-            pltpu.VMEM((256, wide), BF16),
-            pltpu.VMEM((256, hidden), BF16),
+            pltpu.VMEM((128, wide), BF16),
+            pltpu.VMEM((128, hidden), BF16),
             pltpu.VMEM((HD, 512), F32),
             dma((8,)),
             dma,
@@ -578,7 +576,7 @@
             dma((16,)),
             dma((3,)),
             dma,
-            dma((2,)),
+            dma((4,)),
             dma,
             dma((8,)),
             dma((4, 2)),

time: 92.7 us -> 91.3 us (0.985)
  no operation moved by 1% of the time
where the time goes in v5:
time: 91.3 us; the launch traced here: 91.1 us
  Pallas kernels  90.5 us (99%)
    pallas_call x1, Pallas kernels, shards(): pl.pallas_call(layer, out_shape=(jax.ShapeDtypeStruct((8, 2, 32, HD), BF1...  88.8 us

profile of v5, /device:TPU:1, one launch (start us, length us, event | category | flops | bytes accessed | tf_op | source)
XLA Modules:
  0.0 91.1 jit_solution(11821036474707961369)
XLA Ops:
  0.6 88.8 %layer.1 = (bf16[8,2,32,128]{3,2,1,0:T(8,128)(2,1)}, bf16[512,128]{1,0:T(8,128)(2,1)}) custom-call(bf16[32,4096]{1,0:T(8,128)(2,1)} %q_ref.1, bf16[2048,1024]{1,0:T(8,128)(2,1)} %bitcast.8, s32[8,32]{1,0:T(8,128)} %bitcast.13, s32[1,32]{1,0:T(1,128)} %bitcast.14, bf16[8,2,32,128]{3,2,1,0:T(8,128)(2,1)} %bitcast.9, bf16[4096,128]{1,0:T(8,128)(2,1)} %w_hbm.1, ...), custom_call_target="tpu_custom_call" | custom-call | tf_op jit(solution)/shard_map/layer/pallas_call | solution.py:533
  89.4 1.7 %hand_over.1 = (bf16[512,128]{1,0:T(8,128)(2,1)}, bf16[512,128]{1,0:T(8,128)(2,1)}) custom-call(bf16[512,128]{1,0:T(8,128)(2,1)} %bitcast.10, bf16[512,128]{1,0:T(8,128)(2,1)} %get-tuple-element.5.b_ref), custom_call_target="tpu_custom_call" | custom-call | tf_op jit(solution)/shard_map/hand_over/pallas_call | solution.py:603
